TPU v7x, 32 devices: a whole 2x2x4 slice. The times are simulated.
32 devices in a mesh: wide: 16 (over z, y, core), shard: 2 (over x).
Axes of the slice: x: 2, y: 2, z: 4, core: 2. Of those that a mesh axis runs over, the one named last changes fastest.
Arguments:
- weights: bfloat16 [256, 8192], P('shard'), may hold values from -6 to 6
- momentum: bfloat16 [16, 256, 8192], P('wide', 'shard'), may hold values from -6 to 6
- grads: bfloat16 [2, 16, 256, 8192], P(None, 'wide', 'shard'), may hold values from -6 to 6
- offsets: int32 [2, 64], P('shard'), may hold values from 0 to 96
- owners: int32 [2, 64], P('shard'), may hold values from 0 to 63, each once within a row
- exp_avg: float32 [2, 64, 32, 128], P('shard', 'wide'), may hold values from -7 to 7
- exp_sq: float32 [2, 64, 32, 128], P('shard', 'wide'), may hold values from 0.01 to 1
Outputs:
- new_weights: bfloat16 [256, 8192], P('shard')
- new_momentum: bfloat16 [16, 256, 8192], P('wide', 'shard')
- new_avg: float32 [2, 64, 32, 128], P('shard', 'wide')
- new_sq: float32 [2, 64, 32, 128], P('shard', 'wide')
- scales: float32 [2], replicated
Inputs may be any that keep to these rules, and one draw needn't show every extreme that they name: `offsets`: each block's band spans 32 consecutive transform rows. Each row of owners is a permutation of 0 to 63.
All inputs are finite; a program needn't handle non-finite values.
Results may differ from a plain program's by a relative error of at most 0.003.
Values may be sent and summed in bfloat16 or wider, within the bound.
No kernel may reach another device: no remote copies, remote signals or barrier semaphores. Data moves between devices by JAX's collectives and lax.ppermute only.
A program may use at most 128 MiB of HBM per device.

v0:
```python
import jax
import jax.numpy as jnp
import numpy as np
from jax import lax
from jax.experimental import pallas as pl
from jax.experimental.pallas import tpu as pltpu
from jax.sharding import PartitionSpec as P


STEPS = 2

momentum_decay = 0.9
beta_one = 0.8
beta_two = 0.95
adam_eps = 1e-08
rms_eps = 1e-06
learning_rate = 0.2


SMEM = pl.BlockSpec(memory_space=pltpu.SMEM)
VMEM = pl.BlockSpec(memory_space=pltpu.VMEM)
ANY = pl.BlockSpec(memory_space=pl.ANY)
HBM = pl.BlockSpec(memory_space=pltpu.HBM)
SMALL = pltpu.CompilerParams(vmem_limit_bytes=20 << 20)


def dct_table(length):
    frequency = np.arange(length, dtype=np.float64)[:, None]
    position = np.arange(length, dtype=np.float64)[None, :]
    cosines = np.cos(np.pi * (2.0 * position + 1.0) * frequency / (2.0 * length))
    scaling = np.where(frequency == 0.0, np.sqrt(1.0 / length), np.sqrt(2.0 / length))
    return (cosines * scaling).astype(np.float32)


def split_table(table):
    high = table.astype(jnp.bfloat16)
    low = (table - high.astype(np.float32)).astype(jnp.bfloat16)
    return high, low


def row_tables(table):
    high, low = split_table(table)
    decayed_high, decayed_low = split_table(np.float32(momentum_decay) * table)
    wide = table.astype(np.float64)
    residue = momentum_decay * (np.eye(len(table)) - wide @ wide.T)
    parts = (high, low, decayed_high, decayed_low, residue.astype(np.float32).astype(jnp.bfloat16))
    return np.stack([part.astype(np.float32) for part in parts])


def column_tables(table):
    high, low = split_table(table)
    zero = np.zeros_like(low)
    rights = [np.block([[h, l], [h, zero]]) for h, l in ((high, low), (high.T, low.T))]
    lefts = np.block([[high.T, high.T], [low.T, zero]])
    return np.stack([*rights, lefts])


def near_memory(value):
    return pltpu.with_memory_space_constraint(value, pltpu.VMEM)


def far_memory(value):
    return pltpu.with_memory_space_constraint(value, pltpu.HBM)


def halves(value):
    high = value.astype(jnp.bfloat16)
    return high, (value - high.astype(jnp.float32)).astype(jnp.bfloat16)


def dot(left, right):
    return jnp.dot(left, right, preferred_element_type=jnp.float32)


def right_dot(left, table):
    length = left.shape[1]
    both = dot(jnp.concatenate(halves(left), 1), table)
    return both[:, :length] + both[:, length:]


def block_of(part, chunks, row_blocks):
    return (0, part) if row_blocks == 1 else (part // chunks, part % chunks)


def fill_groups(groups_ref, orders):
    for role, order in enumerate(orders):
        for relative in range(1 << len(order)):
            place = 0
            for bit in order:
                place = place * 2 + ((relative >> bit) & 1)
            groups_ref[role, relative] = place


def slot_places(groups_ref, slot, device, row, row_blocks, owned):
    if owned & (owned - 1) == 0:
        relative = (slot >> (owned.bit_length() - 1)) ^ device
        within = slot & (owned - 1)
    else:
        relative = lax.div(slot, owned) ^ device
        within = lax.rem(slot, owned)
    role = device & 1
    within = row * owned + within
    size = row_blocks * owned
    return groups_ref[role, relative] * size + within, groups_ref[1 - role, relative ^ 1] * size + within


def bands(momentum, grads, offsets, owners, picks, columns, band_rows, orders, width):
    row_blocks, col_blocks = offsets.shape
    block_len = picks.shape[-1]
    owned = col_blocks >> len(orders[0])
    slots = row_blocks * col_blocks
    chunks = col_blocks // width
    span = width * block_len

    def kernel(offsets_hbm, owners_hbm, momentum_hbm, grads_hbm, picks_hbm, columns_hbm, momentum_ref, grads_ref, taken_ref,
               keep_ref, send_ref, offsets_ref, owners_ref, groups_ref, picks_ref, columns_ref, lefts, tables, arrivals, *scatters):
        device = lax.axis_index("wide")
        first_role = (device & 1) == 0
        small = [
            pltpu.make_async_copy(source, target, tables.at[index])
            for index, (source, target) in enumerate([
                (offsets_hbm, offsets_ref), (owners_hbm, owners_ref), (picks_hbm, picks_ref), (columns_hbm, columns_ref)])
        ]
        for copy in small:
            copy.start()

        def arrival(part):
            row, chunk = block_of(part, chunks, row_blocks)
            rows = pl.ds(row * block_len, block_len)
            lanes = pl.ds(chunk * span, span)
            return [
                pltpu.make_async_copy(momentum_hbm.at[rows, lanes], momentum_ref.at[rows, lanes], arrivals.at[0, part]),
                pltpu.make_async_copy(grads_hbm.at[:, rows, lanes], grads_ref.at[:, rows, lanes], arrivals.at[1, part]),
            ]

        for part in range(row_blocks * chunks):
            for copy in arrival(part):
                copy.start()
        fill_groups(groups_ref, orders)
        blank = jnp.zeros((band_rows, block_len), jnp.float32)
        for scatter in scatters:
            scatter[...] = jnp.zeros_like(scatter)
        for copy in small:
            copy.wait()

        def body(part, carry):
            for copy in arrival(part):
                copy.wait()
            row, chunk = block_of(part, chunks, row_blocks)
            block_rows = slice(0, block_len) if row_blocks == 1 else pl.ds(pl.multiple_of(row * block_len, block_len), block_len)
            taken_start = part * width * band_rows
            ranges = [pl.ds(offsets_ref[row, chunk * width + index], band_rows) for index in range(width)]
            columns_of = [
                pl.ds(pl.multiple_of((chunk * width + index) * block_len, block_len), block_len) for index in range(width)]
            for index, (rows, lanes) in enumerate(zip(ranges, columns_of)):
                high, low, decayed_high, decayed_low = [picks_ref[number, rows, :].astype(jnp.bfloat16) for number in range(4)]
                first = jnp.concatenate(
                    [jnp.concatenate([decayed_high, high], 1), jnp.concatenate([decayed_low, low], 1)], 0)
                pair = dot(first, jnp.concatenate([momentum_ref[block_rows, lanes], grads_ref[0, block_rows, lanes]], 0))
                left = pair[:band_rows] + pair[band_rows:]
                scatters[index][rows, :] = left
                lefts[index * band_rows:(index + 1) * band_rows, :] = left
            for index, (rows, lanes) in enumerate(zip(ranges, columns_of)):
                high, low, residue = [picks_ref[number, rows, :].astype(jnp.bfloat16) for number in (0, 1, 4)]
                second = jnp.concatenate(
                    [jnp.concatenate([high, residue], 1), jnp.concatenate([low, jnp.zeros_like(low)], 1)], 0)
                pair = dot(second, jnp.concatenate(
                    [grads_ref[1, block_rows, lanes], scatters[index][...].astype(jnp.bfloat16)], 0))
                scatters[index][rows, :] = blank
                left = pair[:band_rows] + pair[band_rows:]
                lefts[(width + index) * band_rows:(width + index + 1) * band_rows, :] = left
                taken_ref[pl.ds(pl.multiple_of(taken_start + index * band_rows, band_rows), band_rows), :] = (
                    momentum_decay * lefts[index * band_rows:(index + 1) * band_rows, :] + left)
            band = right_dot(lefts[...], columns_ref[1])
            for index in range(width):
                slot = owners_ref[row, chunk * width + index]
                here, there = slot_places(groups_ref, slot, device, row, row_blocks, owned)
                values = [band[(step_index * width + index) * band_rows:(step_index * width + index + 1) * band_rows]
                          for step_index in range(STEPS)]
                keep_ref[here] = jnp.where(first_role, values[0], values[1])
                send_ref[there] = jnp.where(first_role, values[1], values[0]).astype(jnp.bfloat16)
            return carry

        lax.fori_loop(0, row_blocks * chunks, body, 0)

    shape = (slots, band_rows, block_len)
    return pl.pallas_call(
        kernel,
        in_specs=[HBM] * 6,
        out_specs=[VMEM] * 5,
        out_shape=[
            pltpu.VMEM(momentum.shape, momentum.dtype),
            pltpu.VMEM(grads.shape, grads.dtype),
            pltpu.VMEM((slots * band_rows, block_len), jnp.float32),
            pltpu.VMEM(shape, jnp.float32),
            pltpu.VMEM(shape, jnp.bfloat16),
        ],
        scratch_shapes=[
            pltpu.SMEM(offsets.shape, offsets.dtype),
            pltpu.SMEM(owners.shape, owners.dtype),
            pltpu.SMEM((STEPS, 1 << len(orders[0])), jnp.int32),
            pltpu.VMEM(picks.shape, picks.dtype),
            pltpu.VMEM(columns.shape, columns.dtype),
            pltpu.VMEM((STEPS * width * band_rows, block_len), jnp.float32),
            pltpu.SemaphoreType.DMA((4,)),
            pltpu.SemaphoreType.DMA((2, row_blocks * chunks)),
        ] + [pltpu.VMEM((block_len, block_len), jnp.float32)] * width,
        compiler_params=SMALL,
        name="bands",
    )(*map(far_memory, (offsets, owners, momentum, grads, picks, columns)))


def left_dot(columns_ref, scatters, ranges, values):
    blank = jnp.zeros_like(values[0])
    highs = []
    lows = []
    for (high_ref, low_ref), rows, value in zip(scatters, ranges, values):
        high = value.astype(jnp.bfloat16).astype(jnp.float32)
        high_ref[rows, :] = high
        low_ref[rows, :] = value - high
        highs.append(high_ref[...].astype(jnp.bfloat16))
        lows.append(low_ref[...].astype(jnp.bfloat16))
        high_ref[rows, :] = blank
        low_ref[rows, :] = blank
    high = jnp.concatenate(highs, 1)
    low = jnp.concatenate(lows, 1)
    length = high.shape[0]
    return dot(columns_ref[2, :length], jnp.concatenate([high, low], 0)) + dot(columns_ref[2, length:, :length], high)


def clear(scatters):
    for part in scatters:
        part[...] = jnp.zeros_like(part)
    return list(zip(scatters[::2], scatters[1::2]))


def momentum_update(momentum, grads, taken, offsets, columns, band_rows, width):
    row_blocks, col_blocks = offsets.shape
    block_len = columns.shape[-1] // 2
    chunks = col_blocks // width
    span = width * block_len

    def kernel(offsets_ref, momentum_ref, grads_ref, taken_ref, columns_ref, out_ref, *scatters):
        scatters = clear(scatters)

        def body(part, carry):
            row, chunk = block_of(part, chunks, row_blocks)
            ranges = [pl.ds(offsets_ref[row, chunk * width + index], band_rows) for index in range(width)]
            values = [
                taken_ref[pl.ds(pl.multiple_of((part * width + index) * band_rows, band_rows), band_rows), :]
                for index in range(width)]
            inverse = left_dot(columns_ref, scatters, ranges, values)
            tile = (pl.ds(pl.multiple_of(row * block_len, block_len), block_len),
                    pl.ds(pl.multiple_of(chunk * span, span), span))
            blended = momentum_decay * momentum_ref[tile].astype(jnp.float32) + grads_ref[(0,) + tile].astype(jnp.float32)
            blended = momentum_decay * blended + grads_ref[(1,) + tile].astype(jnp.float32)
            out_ref[tile] = (blended - inverse).astype(out_ref.dtype)
            return carry

        lax.fori_loop(0, row_blocks * chunks, body, 0)

    return pl.pallas_call(
        kernel,
        in_specs=[SMEM] + [VMEM] * 4,
        out_specs=VMEM,
        out_shape=pltpu.VMEM(momentum.shape, momentum.dtype),
        scratch_shapes=[pltpu.VMEM((block_len, block_len), jnp.float32)] * (2 * width),
        compiler_params=SMALL,
        name="momentum_update",
    )(offsets, *map(near_memory, (momentum, grads, taken, columns)))


def adam(mine, got, exp_avg, exp_sq, replicas):
    flat = exp_avg.shape
    block_len = flat[-1]

    def kernel(mine_ref, got_ref, avg_ref, sq_ref, avg_out, sq_out, raw_keep, raw_send, power_keep, power_send):
        first_role = (lax.axis_index("wide") & 1) == 0
        own = mine_ref[...]
        other = got_ref[...]
        avg = avg_ref[...]
        sq = sq_ref[...]
        raws = []
        powers = []
        for total in (jnp.where(first_role, own, other), jnp.where(first_role, other, own)):
            mean_band = total / replicas
            avg = beta_one * avg + (1.0 - beta_one) * mean_band
            sq = beta_two * sq + (1.0 - beta_two) * mean_band * mean_band
            raw = avg / (jnp.sqrt(sq) + adam_eps)
            raws.append(raw)
            powers.append(jnp.sum((raw * raw).reshape(-1, 8, block_len), axis=0))
        avg_out[...] = avg
        sq_out[...] = sq
        raw_keep[...] = jnp.where(first_role, raws[0], raws[1]).astype(jnp.bfloat16)
        raw_send[...] = jnp.where(first_role, raws[1], raws[0]).astype(jnp.bfloat16)
        power_keep[...] = jnp.where(first_role, powers[0], powers[1])
        power_send[...] = jnp.where(first_role, powers[1], powers[0])

    return pl.pallas_call(
        kernel,
        in_specs=[VMEM] * 4,
        out_specs=[VMEM] * 6,
        out_shape=[pltpu.VMEM(flat, jnp.float32)] * 2 + [pltpu.VMEM(flat, jnp.bfloat16)] * 2
        + [pltpu.VMEM((8, block_len), jnp.float32)] * 2,
        compiler_params=SMALL,
        name="adam",
    )(*map(near_memory, (mine, got, exp_avg, exp_sq)))


def weights_update(weights, pieces, powers, count_all, offsets, owners, columns, ready, orders, width):
    row_blocks, col_blocks = offsets.shape
    block_len = columns.shape[-1] // 2
    half, band_rows, _ = pieces[0].shape
    owned = col_blocks >> len(orders[0])
    chunks = col_blocks // width
    span = width * block_len
    count = len(ready)

    def kernel(offsets_ref, owners_ref, own_power, other_power, weights_ref, columns_ref, *refs):
        piece_refs, ready_refs = refs[:2 * STEPS], refs[2 * STEPS:2 * STEPS + count]
        refs = refs[2 * STEPS + count:]
        out_hbm, scales_ref, ready_hbm = refs[0], refs[1], refs[2:2 + count]
        groups_ref, out_ref, departures, leaving, *scatters = refs[2 + count:]
        device = lax.axis_index("wide")
        first_role = (device & 1) == 0
        copies = [
            pltpu.make_async_copy(source, target, leaving.at[index])
            for index, (source, target) in enumerate(zip(ready_refs, ready_hbm))
        ]
        for copy in copies:
            copy.start()
        fill_groups(groups_ref, orders)
        scatters = clear(scatters)
        scales = [
            jnp.broadcast_to(jnp.sqrt(jnp.sum(power[...], keepdims=True) / count_all + rms_eps), (1, block_len))
            for power in (own_power, other_power)]
        scales_ref[0] = jnp.where(first_role, scales[0], scales[1])[0, 0]
        scales_ref[1] = jnp.where(first_role, scales[1], scales[0])[0, 0]
        factors = [jnp.broadcast_to(1.0 / scale, (band_rows, block_len)) for scale in scales]

        def tile_of(part):
            row, chunk = block_of(part, chunks, row_blocks)
            return (pl.ds(pl.multiple_of(row * block_len, block_len), block_len),
                    pl.ds(pl.multiple_of(chunk * span, span), span))

        def departure(part):
            tile = tile_of(part)
            return pltpu.make_async_copy(out_ref.at[tile], out_hbm.at[tile], departures.at[part])

        def body(part, carry):
            row, chunk = block_of(part, chunks, row_blocks)
            totals = []
            for index in range(width):
                slot = owners_ref[row, chunk * width + index]
                places = slot_places(groups_ref, slot, device, row, row_blocks, owned)
                total = jnp.zeros((band_rows, block_len), jnp.float32)
                for number, place in enumerate(places):
                    is_near = place < half
                    entry = jnp.where(is_near, place, place - half)
                    raw = jnp.where(is_near, piece_refs[2 * number][entry], piece_refs[2 * number + 1][entry])
                    total = total + raw.astype(jnp.float32) * factors[number]
                totals.append(total)
            right = right_dot(jnp.concatenate(totals, 0), columns_ref[0])
            ranges = [pl.ds(offsets_ref[row, chunk * width + index], band_rows) for index in range(width)]
            values = [right[index * band_rows:(index + 1) * band_rows] for index in range(width)]
            inverse = left_dot(columns_ref, scatters, ranges, values)
            tile = tile_of(part)
            out_ref[tile] = (weights_ref[tile].astype(jnp.float32) - learning_rate * inverse).astype(out_ref.dtype)
            departure(part).start()
            return carry

        lax.fori_loop(0, row_blocks * chunks, body, 0)
        for part in range(row_blocks * chunks):
            departure(part).wait()
        for copy in copies:
            copy.wait()

    return pl.pallas_call(
        kernel,
        in_specs=[SMEM, SMEM] + [VMEM] * (4 + 2 * STEPS + count),
        out_specs=[HBM, SMEM] + [HBM] * count,
        out_shape=[
            pltpu.HBM(weights.shape, weights.dtype),
            jax.ShapeDtypeStruct((STEPS,), jnp.float32),
        ] + [pltpu.HBM(value.shape, value.dtype) for value in ready],
        scratch_shapes=[
            pltpu.SMEM((STEPS, 1 << len(orders[0])), jnp.int32),
            pltpu.VMEM(weights.shape, weights.dtype),
            pltpu.SemaphoreType.DMA((row_blocks * chunks,)),
            pltpu.SemaphoreType.DMA((count,)),
        ] + [pltpu.VMEM((block_len, block_len), jnp.float32)] * (2 * width),
        compiler_params=SMALL,
        name="weights_update",
    )(offsets, owners, *map(near_memory, (*powers, weights, columns, *pieces, *ready)))


def swap(value, orders, stage):
    pairs = [(index, index ^ (1 << orders[index & 1][stage])) for index in range(1 << len(orders[0]))]
    return lax.ppermute(value, "wide", pairs)


def across(value, orders, stage, shift, shards):
    pairs = []
    for index in range(1 << len(orders[0])):
        partner = index if stage is None else index ^ (1 << orders[index & 1][stage])
        pairs += [(index * shards + shard, partner * shards + (shard ^ shift)) for shard in range(shards)]
    return lax.ppermute(value, ("wide", "shard"), pairs)


def tree_sum(values):
    while len(values) > 1:
        values = [a + b for a, b in zip(values[::2], values[1::2])]
    return values[0]


def per_device(weights, momentum, grads, offsets, owners, exp_avg, exp_sq):
    row_blocks, owned, band_rows, block_len = exp_avg.shape
    replicas = lax.axis_size("wide")
    shards = lax.axis_size("shard")
    count_all = exp_avg.size * replicas * shards
    table = dct_table(block_len)
    picks = jnp.asarray(row_tables(table))
    columns = jnp.asarray(column_tables(table))
    width = 16
    bits = replicas.bit_length() - 1
    orders = [list(range(1, bits)) + [0] for _ in range(STEPS)]
    if bits > 3:
        orders[1][:2] = orders[1][1::-1]
    core = bits - 1
    near_momentum, near_grads, taken, kept, sent = bands(
        momentum[0], grads[:, 0], offsets, owners, picks, columns, band_rows, orders, width)
    new_momentum = momentum_update(near_momentum, near_grads, taken, offsets, columns, band_rows, width)
    got = swap(sent, orders, core)
    kept = kept + got.astype(jnp.float32)
    for stage in range(core):
        middle = kept.shape[0] // 2
        got = swap(kept[middle:].astype(jnp.bfloat16), orders, stage)
        kept = kept[:middle] + got.astype(jnp.float32)
    middle = kept.shape[0] // 2
    got = swap(kept[middle:], orders, core)
    flat = (row_blocks * owned, band_rows, block_len)
    avg_now, sq_now, raw, raw_other, power, power_other = adam(
        kept[:middle], got, exp_avg.reshape(flat), exp_sq.reshape(flat), replicas)
    far = swap(raw_other, orders, core)
    power_far = swap(power_other, orders, core)
    near = jnp.concatenate([raw, far], 0)
    power = power + power_far
    for stage in reversed(range(core)):
        far = swap(near, orders, stage)
        others = [swap(power, orders, stage)]
        if stage == core - 1:
            for shift in range(1, shards):
                others += [across(power, orders, None, shift, shards), across(power, orders, stage, shift, shards)]
        far, others = lax.optimization_barrier((far, others))
        power = tree_sum([power] + others)
        if stage > 0:
            near = jnp.concatenate([near, far], 0)
    pieces = [near, far, swap(near, orders, core), swap(far, orders, core)]
    powers = [power, swap(power, orders, core)]
    new_weights, scales, new_momentum, avg_now, sq_now = weights_update(
        weights, pieces, powers, count_all, offsets, owners, columns, (new_momentum, avg_now, sq_now), orders, width)
    return (new_weights, new_momentum[None], avg_now.reshape(exp_avg.shape), sq_now.reshape(exp_sq.shape), scales)


def solution(mesh):
    in_specs = (
        P("shard", None),
        P("wide", "shard", None),
        P(None, "wide", "shard", None),
        P("shard", None),
        P("shard", None),
        P("shard", "wide", None, None),
        P("shard", "wide", None, None),
    )
    out_specs = (
        P("shard", None),
        P("wide", "shard", None),
        P("shard", "wide", None, None),
        P("shard", "wide", None, None),
        P(),
    )
    return jax.shard_map(per_device, mesh=mesh, in_specs=in_specs, out_specs=out_specs, check_vma=False)
```

profile of v0, /device:TPU:0, one launch (start us, length us, event | category | flops | bytes accessed | tf_op | source)
XLA Modules:
  0.0 62.4 jit_solution(6212447880846231126)
XLA Ops:
  0.6 6.5 %bands.1 = (bf16[128,8192]{1,0:T(8,128)(2,1)S(1)}, bf16[2,128,8192]{2,1,0:T(8,128)(2,1)S(1)}, f32[2048,128]{1,0:T(8,128)S(1)}, f32[64,32,128]{2,1,0:T(8,128)S(1)}, bf16[64,32,128]{2,1,0:T(8,128)(2,1)S(1)}) custom-call(s32[1,64]{1,0:T(1,128)} %offsets_ref.3, s32[1,64]{1,0:T(1,128)} %owners_ref.1, bf16[128,8192]{1,0:T(8,128)(2,1)} %bitcast.10, ...), custom_call_target="tpu_custom_call" | custom-call | tf_op jit(solution)/shard_map/bands/pallas_call | solution.py:187
  7.2 0.6 collective-permute-start
  7.7 1.5 %collective-permute-done = bf16[64,32,128]{2,1,0:T(8,128)(2,1)S(1)} collective-permute-done((bf16[64,32,128]{2,1,0:T(8,128)(2,1)S(1)}, bf16[64,32,128]{2,1,0:T(8,128)(2,1)S(1)}, u32[]{:S(2)}, u32[]{:S(2)}) %collective-permute-start) | collective-permute-done | bytes 524320 | tf_op jit(solution)/shard_map/ppermute | solution.py:399
  9.3 0.2 convert_add_fusion
  9.5 2.9 %collective-permute-start.1 = (bf16[32,32,128]{2,1,0:T(8,128)(2,1)S(1)}, bf16[32,32,128]{2,1,0:T(8,128)(2,1)S(1)}, u32[]{:S(2)}, u32[]{:S(2)}) collective-permute-start(bf16[32,32,128]{2,1,0:T(8,128)(2,1)S(1)} %slice.49), channel_id=1, source_target_pairs={{0,4},{2,10},{4,0},{6,14},{8,12},{10,2},{12,8},{14,6},{16,20},{18,... | collective-permute-start | bytes 786440 | tf_op jit(solution)/shard_map/ppermute | solution.py:399
  12.5 4.4 %collective-permute-done.1 = bf16[32,32,128]{2,1,0:T(8,128)(2,1)S(1)} collective-permute-done((bf16[32,32,128]{2,1,0:T(8,128)(2,1)S(1)}, bf16[32,32,128]{2,1,0:T(8,128)(2,1)S(1)}, u32[]{:S(2)}, u32[]{:S(2)}) %collective-permute-start.1) | collective-permute-done | bytes 262176 | tf_op jit(solution)/shard_map/ppermute | solution.py:399
  16.8 0.1 slice_add_fusion
  16.9 2.1 %collective-permute-start.2 = (bf16[16,32,128]{2,1,0:T(8,128)(2,1)S(1)}, bf16[16,32,128]{2,1,0:T(8,128)(2,1)S(1)}, u32[]{:S(2)}, u32[]{:S(2)}) collective-permute-start(bf16[16,32,128]{2,1,0:T(8,128)(2,1)S(1)} %slice.50), channel_id=1, source_target_pairs={{0,8},{2,6},{4,12},{6,2},{8,0},{10,14},{12,4},{14,10},{16,24},{18,... | collective-permute-start | bytes 393224 | tf_op jit(solution)/shard_map/ppermute | solution.py:399
  19.1 2.9 %collective-permute-done.2 = bf16[16,32,128]{2,1,0:T(8,128)(2,1)S(1)} collective-permute-done((bf16[16,32,128]{2,1,0:T(8,128)(2,1)S(1)}, bf16[16,32,128]{2,1,0:T(8,128)(2,1)S(1)}, u32[]{:S(2)}, u32[]{:S(2)}) %collective-permute-start.2) | collective-permute-done | bytes 131104 | tf_op jit(solution)/shard_map/ppermute | solution.py:399
  22.1 3.1 %collective-permute-start.3 = (bf16[8,32,128]{2,1,0:T(8,128)(2,1)S(1)}, bf16[8,32,128]{2,1,0:T(8,128)(2,1)S(1)}, u32[]{:S(2)}, u32[]{:S(2)}) collective-permute-start(bf16[8,32,128]{2,1,0:T(8,128)(2,1)S(1)} %slice.51), channel_id=1, source_target_pairs={{0,16},{2,18},{4,20},{6,22},{8,24},{10,26},{12,28},{14,30},{16,0},... | collective-permute-start | bytes 196616 | tf_op jit(solution)/shard_map/ppermute | solution.py:399
  25.1 2.2 %collective-permute-done.3 = bf16[8,32,128]{2,1,0:T(8,128)(2,1)S(1)} collective-permute-done((bf16[8,32,128]{2,1,0:T(8,128)(2,1)S(1)}, bf16[8,32,128]{2,1,0:T(8,128)(2,1)S(1)}, u32[]{:S(2)}, u32[]{:S(2)}) %collective-permute-start.3) | collective-permute-done | bytes 65568 | tf_op jit(solution)/shard_map/ppermute | solution.py:399
  27.4 0.1 collective-permute-start.4
  27.5 1.2 %collective-permute-done.4.got_ref = f32[4,32,128]{2,1,0:T(8,128)S(1)} collective-permute-done((f32[4,32,128]{2,1,0:T(8,128)S(1)}, f32[4,32,128]{2,1,0:T(8,128)S(1)}, u32[]{:S(2)}, u32[]{:S(2)}) %collective-permute-start.4) | collective-permute-done | bytes 65568 | tf_op jit(solution)/shard_map/ppermute | solution.py:399
  28.8 0.1 adam.1
  28.9 0.2 collective-permute-start.5
  29.1 0.4 collective-permute-start.6
  29.5 0.7 %collective-permute-done.5 = f32[8,128]{1,0:T(8,128)S(1)} collective-permute-done((f32[8,128]{1,0:T(8,128)S(1)}, f32[8,128]{1,0:T(8,128)S(1)}, u32[]{:S(2)}, u32[]{:S(2)}) %collective-permute-start.5) | collective-permute-done | bytes 4128 | tf_op jit(solution)/shard_map/ppermute | solution.py:399
  30.1 3.9 %collective-permute-start.10 = (f32[8,128]{1,0:T(8,128)S(1)}, f32[8,128]{1,0:T(8,128)S(1)}, u32[]{:S(2)}, u32[]{:S(2)}) collective-permute-start(f32[8,128]{1,0:T(8,128)S(1)} %add.34), channel_id=1, source_target_pairs={{0,17},{1,16},{2,19},{3,18},{4,21},{5,20},{6,23},{7,22},{8,25},{9,... | collective-permute-start | bytes 12296 | tf_op jit(solution)/shard_map/ppermute | solution.py:407
  34.0 0.6 collective-permute-start.9
  34.6 3.0 %collective-permute-start.7 = (bf16[8,32,128]{2,1,0:T(8,128)(2,1)S(1)}, bf16[8,32,128]{2,1,0:T(8,128)(2,1)S(1)}, u32[]{:S(2)}, u32[]{:S(2)}) collective-permute-start(bf16[8,32,128]{2,1,0:T(8,128)(2,1)S(1)} %pad_maximum_fusion.1), channel_id=1, source_target_pairs={{0,16},{2,18},{4,20},{6,22},{8,24},{10,26},{12,28},{14,30},{16,0},... | collective-permute-start | bytes 196616 | tf_op jit(solution)/shard_map/ppermute | solution.py:399
  37.6 0.0 collective-permute-done.9
  37.6 1.5 %collective-permute-done.8 = f32[8,128]{1,0:T(8,128)S(1)} collective-permute-done((f32[8,128]{1,0:T(8,128)S(1)}, f32[8,128]{1,0:T(8,128)S(1)}, u32[]{:S(2)}, u32[]{:S(2)}) %collective-permute-start.8) | collective-permute-done | bytes 4128 | tf_op jit(solution)/shard_map/ppermute | solution.py:399
  39.1 1.5 %collective-permute-done.7 = bf16[8,32,128]{2,1,0:T(8,128)(2,1)S(1)} collective-permute-done((bf16[8,32,128]{2,1,0:T(8,128)(2,1)S(1)}, bf16[8,32,128]{2,1,0:T(8,128)(2,1)S(1)}, u32[]{:S(2)}, u32[]{:S(2)}) %collective-permute-start.7) | collective-permute-done | bytes 65568 | tf_op jit(solution)/shard_map/ppermute | solution.py:399
  40.6 1.4 %collective-permute-start.11 = (bf16[16,32,128]{2,1,0:T(8,128)(2,1)S(1)}, bf16[16,32,128]{2,1,0:T(8,128)(2,1)S(1)}, u32[]{:S(2)}, u32[]{:S(2)}) collective-permute-start(bf16[16,32,128]{2,1,0:T(8,128)(2,1)S(1)} %pad_maximum_fusion), channel_id=1, source_target_pairs={{0,8},{2,6},{4,12},{6,2},{8,0},{10,14},{12,4},{14,10},{16,24},{18,... | collective-permute-start | bytes 393224 | tf_op jit(solution)/shard_map/ppermute | solution.py:399
  42.0 0.7 %collective-permute-start.12 = (f32[8,128]{1,0:T(8,128)S(1)}, f32[8,128]{1,0:T(8,128)S(1)}, u32[]{:S(2)}, u32[]{:S(2)}) collective-permute-start(f32[8,128]{1,0:T(8,128)S(1)} %add_add_fusion), channel_id=1, source_target_pairs={{0,8},{2,6},{4,12},{6,2},{8,0},{10,14},{12,4},{14,10},{16,24},{18,... | collective-permute-start | bytes 12296 | tf_op jit(solution)/shard_map/ppermute | solution.py:399
  42.7 3.3 %collective-permute-done.12 = f32[8,128]{1,0:T(8,128)S(1)} collective-permute-done((f32[8,128]{1,0:T(8,128)S(1)}, f32[8,128]{1,0:T(8,128)S(1)}, u32[]{:S(2)}, u32[]{:S(2)}) %collective-permute-start.12) | collective-permute-done | bytes 4128 | tf_op jit(solution)/shard_map/ppermute | solution.py:399
  46.0 3.3 %collective-permute-start.13 = (bf16[32,32,128]{2,1,0:T(8,128)(2,1)S(1)}, bf16[32,32,128]{2,1,0:T(8,128)(2,1)S(1)}, u32[]{:S(2)}, u32[]{:S(2)}) collective-permute-start(bf16[32,32,128]{2,1,0:T(8,128)(2,1)S(1)} %constant_dynamic-update-slice_fusion.refs_0_), channel_id=1, source_target_pairs={{0,4},{2,10},{4,0},{6,14},{8,12},{10,2},{12,8},{14,6},{16,20},{18,... | collective-permute-start | bytes 786440 | tf_op jit(solution)/shard_map/ppermute | solution.py:399
  49.4 0.1 collective-permute-start.14
  49.4 4.3 %collective-permute-done.14 = f32[8,128]{1,0:T(8,128)S(1)} collective-permute-done((f32[8,128]{1,0:T(8,128)S(1)}, f32[8,128]{1,0:T(8,128)S(1)}, u32[]{:S(2)}, u32[]{:S(2)}) %collective-permute-start.14) | collective-permute-done | bytes 4128 | tf_op jit(solution)/shard_map/ppermute | solution.py:399
  53.8 0.5 collective-permute-start.15
  54.3 3.0 %momentum_update.1.refs_4_ = bf16[128,8192]{1,0:T(8,128)(2,1)S(1)} custom-call(s32[1,64]{1,0:T(1,128)S(1)} %copy-done.4, bf16[128,8192]{1,0:T(8,128)(2,1)S(1)} %get-tuple-element.43.momentum_ref, bf16[2,128,8192]{2,1,0:T(8,128)(2,1)S(1)} %get-tuple-element.44.grads_ref, f32[2048,128]{1,0:T(8,128)S(1)} %get-tuple-element.45.taken_ref, ...), custom_call_target="tpu_custom_call" | custom-call | tf_op jit(solution)/shard_map/momentum_update/pallas_call | solution.py:262
  57.3 5.1 %weights_update.1 = (bf16[128,8192]{1,0:T(8,128)(2,1)}, f32[2]{0:T(128)}, bf16[128,8192]{1,0:T(8,128)(2,1)}, f32[4,32,128]{2,1,0:T(8,128)}, f32[4,32,128]{2,1,0:T(8,128)}) custom-call(s32[1,64]{1,0:T(1,128)S(1)} %copy-done.4, s32[1,64]{1,0:T(1,128)S(1)} %copy-done.5, f32[8,128]{1,0:T(8,128)S(1)} %add.39.own_power, ...), custom_call_target="tpu_custom_call" | custom-call | tf_op jit(solution)/shard_map/weights_update/pallas_call | solution.py:378
  (38 shorter events, 0.3 us)
Async XLA Ops:
  7.2 2.1 %collective-permute-start = (bf16[64,32,128]{2,1,0:T(8,128)(2,1)S(1)}, bf16[64,32,128]{2,1,0:T(8,128)(2,1)S(1)}, u32[]{:S(2)}, u32[]{:S(2)}) collective-permute-start(bf16[64,32,128]{2,1,0:T(8,128)(2,1)S(1)} %get-tuple-element.30), channel_id=1, source_target_pairs={{0,2},{2,0},{4,6},{6,4},{8,10},{10,8},{12,14},{14,12},{16,18},{18,... | collective-permute-start | bytes 1572872 | tf_op jit(solution)/shard_map/ppermute | solution.py:399
  9.4 19.3 %copy-start.2 = (f32[1,4,32,128]{3,2,1,0:T(8,128)S(1)}, f32[1,4,32,128]{3,2,1,0:T(8,128)}, u32[]{:S(2)}) copy-start(f32[1,4,32,128]{3,2,1,0:T(8,128)} %param.14) | copy-start | bytes 196612
  9.4 19.3 %copy-start.3 = (f32[1,4,32,128]{3,2,1,0:T(8,128)S(1)}, f32[1,4,32,128]{3,2,1,0:T(8,128)}, u32[]{:S(2)}) copy-start(f32[1,4,32,128]{3,2,1,0:T(8,128)} %param.15) | copy-start | bytes 196612
  9.5 44.8 %copy-start = (bf16[3,256,256]{2,1,0:T(8,128)(2,1)S(1)}, bf16[3,256,256]{2,1,0:T(8,128)(2,1)}, u32[]{:S(2)}) copy-start(bf16[3,256,256]{2,1,0:T(8,128)(2,1)} %constant.5.clone.columns_hbm.columns_ref) | copy-start | bytes 1179652
  9.5 44.8 %copy-start.4 = (s32[1,64]{1,0:T(1,128)S(1)}, s32[1,64]{1,0:T(1,128)}, u32[]{:S(2)}) copy-start(s32[1,64]{1,0:T(1,128)} %offsets_ref.3) | copy-start | bytes 772
  9.5 7.3 %collective-permute-start.1 = (bf16[32,32,128]{2,1,0:T(8,128)(2,1)S(1)}, bf16[32,32,128]{2,1,0:T(8,128)(2,1)S(1)}, u32[]{:S(2)}, u32[]{:S(2)}) collective-permute-start(bf16[32,32,128]{2,1,0:T(8,128)(2,1)S(1)} %slice.49), channel_id=1, source_target_pairs={{0,4},{2,10},{4,0},{6,14},{8,12},{10,2},{12,8},{14,6},{16,20},{18,... | collective-permute-start | bytes 786440 | tf_op jit(solution)/shard_map/ppermute | solution.py:399
  16.9 5.1 %collective-permute-start.2 = (bf16[16,32,128]{2,1,0:T(8,128)(2,1)S(1)}, bf16[16,32,128]{2,1,0:T(8,128)(2,1)S(1)}, u32[]{:S(2)}, u32[]{:S(2)}) collective-permute-start(bf16[16,32,128]{2,1,0:T(8,128)(2,1)S(1)} %slice.50), channel_id=1, source_target_pairs={{0,8},{2,6},{4,12},{6,2},{8,0},{10,14},{12,4},{14,10},{16,24},{18,... | collective-permute-start | bytes 393224 | tf_op jit(solution)/shard_map/ppermute | solution.py:399
  22.1 5.3 %collective-permute-start.3 = (bf16[8,32,128]{2,1,0:T(8,128)(2,1)S(1)}, bf16[8,32,128]{2,1,0:T(8,128)(2,1)S(1)}, u32[]{:S(2)}, u32[]{:S(2)}) collective-permute-start(bf16[8,32,128]{2,1,0:T(8,128)(2,1)S(1)} %slice.51), channel_id=1, source_target_pairs={{0,16},{2,18},{4,20},{6,22},{8,24},{10,26},{12,28},{14,30},{16,0},... | collective-permute-start | bytes 196616 | tf_op jit(solution)/shard_map/ppermute | solution.py:399
  27.4 1.3 %collective-permute-start.4 = (f32[4,32,128]{2,1,0:T(8,128)S(1)}, f32[4,32,128]{2,1,0:T(8,128)S(1)}, u32[]{:S(2)}, u32[]{:S(2)}) collective-permute-start(f32[4,32,128]{2,1,0:T(8,128)S(1)} %get-tuple-element.53), channel_id=1, source_target_pairs={{0,2},{2,0},{4,6},{6,4},{8,10},{10,8},{12,14},{14,12},{16,18},{18,... | collective-permute-start | bytes 196616 | tf_op jit(solution)/shard_map/ppermute | solution.py:399
  28.9 1.2 %collective-permute-start.5 = (f32[8,128]{1,0:T(8,128)S(1)}, f32[8,128]{1,0:T(8,128)S(1)}, u32[]{:S(2)}, u32[]{:S(2)}) collective-permute-start(f32[8,128]{1,0:T(8,128)S(1)} %get-tuple-element.32), channel_id=1, source_target_pairs={{0,2},{2,0},{4,6},{6,4},{8,10},{10,8},{12,14},{14,12},{16,18},{18,... | collective-permute-start | bytes 12296 | tf_op jit(solution)/shard_map/ppermute | solution.py:399
  29.1 5.5 %collective-permute-start.6 = (bf16[4,32,128]{2,1,0:T(8,128)(2,1)S(1)}, bf16[4,32,128]{2,1,0:T(8,128)(2,1)S(1)}, u32[]{:S(2)}, u32[]{:S(2)}) collective-permute-start(bf16[4,32,128]{2,1,0:T(8,128)(2,1)S(1)} %get-tuple-element.34), channel_id=1, source_target_pairs={{0,2},{2,0},{4,6},{6,4},{8,10},{10,8},{12,14},{14,12},{16,18},{18,... | collective-permute-start | bytes 98312 | tf_op jit(solution)/shard_map/ppermute | solution.py:399
  30.1 7.5 %collective-permute-start.10 = (f32[8,128]{1,0:T(8,128)S(1)}, f32[8,128]{1,0:T(8,128)S(1)}, u32[]{:S(2)}, u32[]{:S(2)}) collective-permute-start(f32[8,128]{1,0:T(8,128)S(1)} %add.34), channel_id=1, source_target_pairs={{0,17},{1,16},{2,19},{3,18},{4,21},{5,20},{6,23},{7,22},{8,25},{9,... | collective-permute-start | bytes 12296 | tf_op jit(solution)/shard_map/ppermute | solution.py:407
  34.0 3.6 %collective-permute-start.9 = (f32[8,128]{1,0:T(8,128)S(1)}, f32[8,128]{1,0:T(8,128)S(1)}, u32[]{:S(2)}, u32[]{:S(2)}) collective-permute-start(f32[8,128]{1,0:T(8,128)S(1)} %add.34), channel_id=1, source_target_pairs={{0,1},{1,0},{2,3},{3,2},{4,5},{5,4},{6,7},{7,6},{8,9},{9,8},{10,11... | collective-permute-start | bytes 12296 | tf_op jit(solution)/shard_map/ppermute | solution.py:407
  34.6 4.5 %collective-permute-start.8 = (f32[8,128]{1,0:T(8,128)S(1)}, f32[8,128]{1,0:T(8,128)S(1)}, u32[]{:S(2)}, u32[]{:S(2)}) collective-permute-start(f32[8,128]{1,0:T(8,128)S(1)} %add.34), channel_id=1, source_target_pairs={{0,16},{2,18},{4,20},{6,22},{8,24},{10,26},{12,28},{14,30},{16,0},... | collective-permute-start | bytes 12296 | tf_op jit(solution)/shard_map/ppermute | solution.py:399
  34.6 6.0 %collective-permute-start.7 = (bf16[8,32,128]{2,1,0:T(8,128)(2,1)S(1)}, bf16[8,32,128]{2,1,0:T(8,128)(2,1)S(1)}, u32[]{:S(2)}, u32[]{:S(2)}) collective-permute-start(bf16[8,32,128]{2,1,0:T(8,128)(2,1)S(1)} %pad_maximum_fusion.1), channel_id=1, source_target_pairs={{0,16},{2,18},{4,20},{6,22},{8,24},{10,26},{12,28},{14,30},{16,0},... | collective-permute-start | bytes 196616 | tf_op jit(solution)/shard_map/ppermute | solution.py:399
  40.6 5.4 %collective-permute-start.11 = (bf16[16,32,128]{2,1,0:T(8,128)(2,1)S(1)}, bf16[16,32,128]{2,1,0:T(8,128)(2,1)S(1)}, u32[]{:S(2)}, u32[]{:S(2)}) collective-permute-start(bf16[16,32,128]{2,1,0:T(8,128)(2,1)S(1)} %pad_maximum_fusion), channel_id=1, source_target_pairs={{0,8},{2,6},{4,12},{6,2},{8,0},{10,14},{12,4},{14,10},{16,24},{18,... | collective-permute-start | bytes 393224 | tf_op jit(solution)/shard_map/ppermute | solution.py:399
  42.0 4.0 %collective-permute-start.12 = (f32[8,128]{1,0:T(8,128)S(1)}, f32[8,128]{1,0:T(8,128)S(1)}, u32[]{:S(2)}, u32[]{:S(2)}) collective-permute-start(f32[8,128]{1,0:T(8,128)S(1)} %add_add_fusion), channel_id=1, source_target_pairs={{0,8},{2,6},{4,12},{6,2},{8,0},{10,14},{12,4},{14,10},{16,24},{18,... | collective-permute-start | bytes 12296 | tf_op jit(solution)/shard_map/ppermute | solution.py:399
  46.0 7.7 %collective-permute-start.13 = (bf16[32,32,128]{2,1,0:T(8,128)(2,1)S(1)}, bf16[32,32,128]{2,1,0:T(8,128)(2,1)S(1)}, u32[]{:S(2)}, u32[]{:S(2)}) collective-permute-start(bf16[32,32,128]{2,1,0:T(8,128)(2,1)S(1)} %constant_dynamic-update-slice_fusion.refs_0_), channel_id=1, source_target_pairs={{0,4},{2,10},{4,0},{6,14},{8,12},{10,2},{12,8},{14,6},{16,20},{18,... | collective-permute-start | bytes 786440 | tf_op jit(solution)/shard_map/ppermute | solution.py:399
  49.4 4.4 %collective-permute-start.14 = (f32[8,128]{1,0:T(8,128)S(1)}, f32[8,128]{1,0:T(8,128)S(1)}, u32[]{:S(2)}, u32[]{:S(2)}) collective-permute-start(f32[8,128]{1,0:T(8,128)S(1)} %add.38), channel_id=1, source_target_pairs={{0,4},{2,10},{4,0},{6,14},{8,12},{10,2},{12,8},{14,6},{16,20},{18,... | collective-permute-start | bytes 12296 | tf_op jit(solution)/shard_map/ppermute | solution.py:399
  49.4 7.8 %collective-permute-start.16 = (bf16[32,32,128]{2,1,0:T(8,128)(2,1)S(1)}, bf16[32,32,128]{2,1,0:T(8,128)(2,1)S(1)}, u32[]{:S(2)}, u32[]{:S(2)}) collective-permute-start(bf16[32,32,128]{2,1,0:T(8,128)(2,1)S(1)} %constant_dynamic-update-slice_fusion.refs_0_), channel_id=1, source_target_pairs={{0,2},{2,0},{4,6},{6,4},{8,10},{10,8},{12,14},{14,12},{16,18},{18,... | collective-permute-start | bytes 786440 | tf_op jit(solution)/shard_map/ppermute | solution.py:399
  53.7 3.5 %collective-permute-start.17 = (bf16[32,32,128]{2,1,0:T(8,128)(2,1)S(1)}, bf16[32,32,128]{2,1,0:T(8,128)(2,1)S(1)}, u32[]{:S(2)}, u32[]{:S(2)}) collective-permute-start(bf16[32,32,128]{2,1,0:T(8,128)(2,1)S(1)} %collective-permute-done.13.refs_1_), channel_id=1, source_target_pairs={{0,2},{2,0},{4,6},{6,4},{8,10},{10,8},{12,14},{14,12},{16,18},{18,... | collective-permute-start | bytes 786440 | tf_op jit(solution)/shard_map/ppermute | solution.py:399
  53.8 3.5 %collective-permute-start.15 = (f32[8,128]{1,0:T(8,128)S(1)}, f32[8,128]{1,0:T(8,128)S(1)}, u32[]{:S(2)}, u32[]{:S(2)}) collective-permute-start(f32[8,128]{1,0:T(8,128)S(1)} %add.39.own_power), channel_id=1, source_target_pairs={{0,2},{2,0},{4,6},{6,4},{8,10},{10,8},{12,14},{14,12},{16,18},{18,... | collective-permute-start | bytes 12296 | tf_op jit(solution)/shard_map/ppermute | solution.py:399
  54.3 3.0 %copy-start.1 = (bf16[128,8192]{1,0:T(8,128)(2,1)S(1)}, bf16[128,8192]{1,0:T(8,128)(2,1)}, u32[]{:S(2)}) copy-start(bf16[128,8192]{1,0:T(8,128)(2,1)} %weights_ref.1) | copy-start | bytes 6291460
  54.3 3.0 %copy-start.5 = (s32[1,64]{1,0:T(1,128)S(1)}, s32[1,64]{1,0:T(1,128)}, u32[]{:S(2)}) copy-start(s32[1,64]{1,0:T(1,128)} %owners_ref.1) | copy-start | bytes 772
where the time goes:
time: 62.6 us; the launch traced here: 62.4 us
  waiting for transfers between devices  23.6 us (38%)
  starting transfers between devices  22.8 us (36%)
  Pallas kernels  14.7 us (23%)
  between operations  0.83 us (1%)
    ppermute x16, waiting for transfers between devices, swap(): return lax.ppermute(value, 'wide', pairs)  23.5 us
    ppermute x16, starting transfers between devices, swap(): return lax.ppermute(value, 'wide', pairs)  18.4 us
    pallas_call x1, Pallas kernels, bands(): pl.pallas_call(kernel, in_specs=[HBM] * 6, out_specs=[VMEM] * 5, out_shap...  6.51 us
    pallas_call x1, Pallas kernels, weights_update(): pl.pallas_call(kernel, in_specs=[SMEM, SMEM] + [VMEM] * (4 + 2 * STEPS +...  5.12 us
    ppermute x2, starting transfers between devices, across(): return lax.ppermute(value, ('wide', 'shard'), pairs)  4.44 us
    pallas_call x1, Pallas kernels, momentum_update(): pl.pallas_call(kernel, in_specs=[SMEM] + [VMEM] * 4, out_specs=VMEM, out_...  2.99 us
  transfers between devices with their start and end apart: 18, of which 10 were waited for; matrix products, arithmetic and copies ran while one was open for 0% of the time, Pallas kernels for 5%

commit v1 on v0

--- a/solution.py
+++ b/solution.py
@@ -8,6 +8,7 @@
 
 
 STEPS = 2
+TILE = 16
 
 momentum_decay = 0.9
 beta_one = 0.8
@@ -91,16 +92,17 @@
             groups_ref[role, relative] = place
 
 
-def slot_places(groups_ref, slot, device, row, row_blocks, owned):
+def owner_of(slot, owned):
     if owned & (owned - 1) == 0:
-        relative = (slot >> (owned.bit_length() - 1)) ^ device
-        within = slot & (owned - 1)
-    else:
-        relative = lax.div(slot, owned) ^ device
-        within = lax.rem(slot, owned)
+        return slot >> (owned.bit_length() - 1), slot & (owned - 1)
+    return lax.div(slot, owned), lax.rem(slot, owned)
+
+
+def slot_places(groups_ref, slot, device, row, owned, size):
+    owner, within = owner_of(slot, owned)
+    relative = owner ^ device
     role = device & 1
     within = row * owned + within
-    size = row_blocks * owned
     return groups_ref[role, relative] * size + within, groups_ref[1 - role, relative ^ 1] * size + within
 
 
@@ -174,7 +176,7 @@
             band = right_dot(lefts[...], columns_ref[1])
             for index in range(width):
                 slot = owners_ref[row, chunk * width + index]
-                here, there = slot_places(groups_ref, slot, device, row, row_blocks, owned)
+                here, there = slot_places(groups_ref, slot, device, row, owned, row_blocks * owned)
                 values = [band[(step_index * width + index) * band_rows:(step_index * width + index + 1) * band_rows]
                           for step_index in range(STEPS)]
                 keep_ref[here] = jnp.where(first_role, values[0], values[1])
@@ -273,56 +275,67 @@
 def adam(mine, got, exp_avg, exp_sq, replicas):
     flat = exp_avg.shape
     block_len = flat[-1]
-
-    def kernel(mine_ref, got_ref, avg_ref, sq_ref, avg_out, sq_out, raw_keep, raw_send, power_keep, power_send):
+    rows = flat[0] * flat[1]
+
+    def kernel(mine_ref, got_ref, avg_ref, sq_ref, avg_out, sq_out, raw_keep, raw_send):
         first_role = (lax.axis_index("wide") & 1) == 0
         own = mine_ref[...]
         other = got_ref[...]
         avg = avg_ref[...]
         sq = sq_ref[...]
+        row = lax.broadcasted_iota(jnp.int32, (TILE, block_len), 0)
+        tile = jnp.zeros((TILE, block_len), jnp.float32)
         raws = []
-        powers = []
-        for total in (jnp.where(first_role, own, other), jnp.where(first_role, other, own)):
+        for step_index, total in enumerate((jnp.where(first_role, own, other), jnp.where(first_role, other, own))):
             mean_band = total / replicas
             avg = beta_one * avg + (1.0 - beta_one) * mean_band
             sq = beta_two * sq + (1.0 - beta_two) * mean_band * mean_band
             raw = avg / (jnp.sqrt(sq) + adam_eps)
-            raws.append(raw)
-            powers.append(jnp.sum((raw * raw).reshape(-1, 8, block_len), axis=0))
+            raws.append(raw.reshape(rows, block_len))
+            rest = jnp.sum(raws[-1] * raws[-1], axis=0, keepdims=True)
+            for part in range(3):
+                piece = rest.astype(jnp.bfloat16).astype(jnp.float32)
+                tile = jnp.where(row == STEPS * part + step_index, piece, tile)
+                rest = rest - piece
         avg_out[...] = avg
         sq_out[...] = sq
-        raw_keep[...] = jnp.where(first_role, raws[0], raws[1]).astype(jnp.bfloat16)
-        raw_send[...] = jnp.where(first_role, raws[1], raws[0]).astype(jnp.bfloat16)
-        power_keep[...] = jnp.where(first_role, powers[0], powers[1])
-        power_send[...] = jnp.where(first_role, powers[1], powers[0])
+        raw_keep[:rows, :] = jnp.where(first_role, raws[0], raws[1]).astype(jnp.bfloat16)
+        raw_send[:rows, :] = jnp.where(first_role, raws[1], raws[0]).astype(jnp.bfloat16)
+        raw_keep[rows:, :] = tile.astype(jnp.bfloat16)
+        raw_send[rows:, :] = tile.astype(jnp.bfloat16)
 
     return pl.pallas_call(
         kernel,
         in_specs=[VMEM] * 4,
-        out_specs=[VMEM] * 6,
-        out_shape=[pltpu.VMEM(flat, jnp.float32)] * 2 + [pltpu.VMEM(flat, jnp.bfloat16)] * 2
-        + [pltpu.VMEM((8, block_len), jnp.float32)] * 2,
+        out_specs=[VMEM] * 4,
+        out_shape=[pltpu.VMEM(flat, jnp.float32)] * 2 + [pltpu.VMEM((rows + TILE, block_len), jnp.bfloat16)] * 2,
         compiler_params=SMALL,
         name="adam",
     )(*map(near_memory, (mine, got, exp_avg, exp_sq)))
 
 
-def weights_update(weights, pieces, powers, count_all, offsets, owners, columns, ready, orders, width):
+def weights_update(weights, own, other, tiles, count_all, offsets, owners, columns, ready, orders, band_rows, width):
     row_blocks, col_blocks = offsets.shape
     block_len = columns.shape[-1] // 2
-    half, band_rows, _ = pieces[0].shape
+    size = own[0].shape[0]
+    pieces = len(own)
+    stride = size * pieces >> len(orders[0])
+    shift = (size // stride).bit_length() - 1
+    shards = tiles.shape[0] + 1
     owned = col_blocks >> len(orders[0])
     chunks = col_blocks // width
     span = width * block_len
     count = len(ready)
 
-    def kernel(offsets_ref, owners_ref, own_power, other_power, weights_ref, columns_ref, *refs):
-        piece_refs, ready_refs = refs[:2 * STEPS], refs[2 * STEPS:2 * STEPS + count]
-        refs = refs[2 * STEPS + count:]
+    def kernel(offsets_ref, owners_ref, tiles_ref, weights_ref, columns_ref, *refs):
+        piece_refs = [refs[:pieces], refs[pieces:2 * pieces]]
+        ready_refs = refs[2 * pieces:2 * pieces + count]
+        refs = refs[2 * pieces + count:]
         out_hbm, scales_ref, ready_hbm = refs[0], refs[1], refs[2:2 + count]
         groups_ref, out_ref, departures, leaving, *scatters = refs[2 + count:]
         device = lax.axis_index("wide")
-        first_role = (device & 1) == 0
+        role = device & 1
+        first_role = role == 0
         copies = [
             pltpu.make_async_copy(source, target, leaving.at[index])
             for index, (source, target) in enumerate(zip(ready_refs, ready_hbm))
@@ -331,12 +344,18 @@
             copy.start()
         fill_groups(groups_ref, orders)
         scatters = clear(scatters)
-        scales = [
-            jnp.broadcast_to(jnp.sqrt(jnp.sum(power[...], keepdims=True) / count_all + rms_eps), (1, block_len))
-            for power in (own_power, other_power)]
-        scales_ref[0] = jnp.where(first_role, scales[0], scales[1])[0, 0]
-        scales_ref[1] = jnp.where(first_role, scales[1], scales[0])[0, 0]
-        factors = [jnp.broadcast_to(1.0 / scale, (band_rows, block_len)) for scale in scales]
+        scales = []
+        rows = [[ref[begin + stride - TILE:begin + stride, :] for ref in piece_refs[0] for begin in range(0, size, stride)]]
+        for shard in range(shards - 1):
+            rows.append([tiles_ref[shard, group] for group in range(1 << len(orders[0]))])
+        tile = tree_sum([axis_sum([value.astype(jnp.float32) for value in values], orders, first_role) for values in rows])
+        parity = lax.broadcasted_iota(jnp.int32, tile.shape, 0) & 1
+        for step_index in range(STEPS):
+            power = jnp.sum(jnp.where(parity == step_index, tile, 0.0), keepdims=True)
+            scales.append(jnp.broadcast_to(jnp.sqrt(power / count_all + rms_eps), (1, block_len)))
+        inverses = [1.0 / scale for scale in scales]
+        factors = [jnp.broadcast_to(factor, (band_rows, block_len)) for factor in (
+            jnp.where(first_role, inverses[0], inverses[1]), jnp.where(first_role, inverses[1], inverses[0]))]
 
         def tile_of(part):
             row, chunk = block_of(part, chunks, row_blocks)
@@ -352,12 +371,16 @@
             totals = []
             for index in range(width):
                 slot = owners_ref[row, chunk * width + index]
-                places = slot_places(groups_ref, slot, device, row, row_blocks, owned)
+                owner, within = owner_of(slot, owned)
+                within = (row * owned + within) * band_rows
                 total = jnp.zeros((band_rows, block_len), jnp.float32)
-                for number, place in enumerate(places):
-                    is_near = place < half
-                    entry = jnp.where(is_near, place, place - half)
-                    raw = jnp.where(is_near, piece_refs[2 * number][entry], piece_refs[2 * number + 1][entry])
+                for number in range(STEPS):
+                    group = groups_ref[role ^ number, owner ^ device ^ number]
+                    which = group >> shift
+                    rows = pl.ds(pl.multiple_of((group & ((1 << shift) - 1)) * stride + within, TILE), band_rows)
+                    raw = piece_refs[number][0][rows, :]
+                    for piece in range(1, pieces):
+                        raw = jnp.where(which == piece, piece_refs[number][piece][rows, :], raw)
                     total = total + raw.astype(jnp.float32) * factors[number]
                 totals.append(total)
             right = right_dot(jnp.concatenate(totals, 0), columns_ref[0])
@@ -370,6 +393,8 @@
             return carry
 
         lax.fori_loop(0, row_blocks * chunks, body, 0)
+        for step_index in range(STEPS):
+            scales_ref[step_index] = scales[step_index][0, 0]
         for part in range(row_blocks * chunks):
             departure(part).wait()
         for copy in copies:
@@ -377,7 +402,7 @@
 
     return pl.pallas_call(
         kernel,
-        in_specs=[SMEM, SMEM] + [VMEM] * (4 + 2 * STEPS + count),
+        in_specs=[SMEM, SMEM] + [VMEM] * (3 + 2 * pieces + count),
         out_specs=[HBM, SMEM] + [HBM] * count,
         out_shape=[
             pltpu.HBM(weights.shape, weights.dtype),
@@ -391,7 +416,7 @@
         ] + [pltpu.VMEM((block_len, block_len), jnp.float32)] * (2 * width),
         compiler_params=SMALL,
         name="weights_update",
-    )(offsets, owners, *map(near_memory, (*powers, weights, columns, *pieces, *ready)))
+    )(offsets, owners, *map(near_memory, (tiles, weights, columns, *own, *other, *ready)))
 
 
 def swap(value, orders, stage):
@@ -405,6 +430,18 @@
         partner = index if stage is None else index ^ (1 << orders[index & 1][stage])
         pairs += [(index * shards + shard, partner * shards + (shard ^ shift)) for shard in range(shards)]
     return lax.ppermute(value, ("wide", "shard"), pairs)
+
+
+def axis_sum(values, orders, first_role):
+    sums = []
+    for order in orders:
+        entries = {}
+        for place, value in enumerate(values):
+            digits = [place >> (len(order) - 1 - position) & 1 for position in range(len(order))]
+            entries[sum(digit << bit for digit, bit in zip(digits, order))] = value
+        current = [entries[index] for index in range(len(values))]
+        sums.append(tree_sum(current))
+    return jnp.where(first_role, *sums)
 
 
 def tree_sum(values):
@@ -432,33 +469,37 @@
     new_momentum = momentum_update(near_momentum, near_grads, taken, offsets, columns, band_rows, width)
     got = swap(sent, orders, core)
     kept = kept + got.astype(jnp.float32)
+    middle = kept.shape[0] // 2
+    keep, send = kept[:middle], kept[middle:]
     for stage in range(core):
-        middle = kept.shape[0] // 2
-        got = swap(kept[middle:].astype(jnp.bfloat16), orders, stage)
-        kept = kept[:middle] + got.astype(jnp.float32)
-    middle = kept.shape[0] // 2
-    got = swap(kept[middle:], orders, core)
+        middle = send.shape[0] // 2
+        if stage == core - 1:
+            keep = keep + swap(send.astype(jnp.bfloat16), orders, stage).astype(jnp.float32)
+            keep, send = keep[:middle], keep[middle:]
+            break
+        high = swap(send[middle:].astype(jnp.bfloat16), orders, stage)
+        low = swap(send[:middle].astype(jnp.bfloat16), orders, stage)
+        send = keep[middle:] + high.astype(jnp.float32)
+        low, _ = lax.optimization_barrier((low, send))
+        keep = keep[:middle] + low.astype(jnp.float32)
+    got = swap(send, orders, core)
     flat = (row_blocks * owned, band_rows, block_len)
-    avg_now, sq_now, raw, raw_other, power, power_other = adam(
-        kept[:middle], got, exp_avg.reshape(flat), exp_sq.reshape(flat), replicas)
+    avg_now, sq_now, raw, raw_other = adam(keep, got, exp_avg.reshape(flat), exp_sq.reshape(flat), replicas)
     far = swap(raw_other, orders, core)
-    power_far = swap(power_other, orders, core)
-    near = jnp.concatenate([raw, far], 0)
-    power = power + power_far
+    nears, fars = [], [jnp.concatenate([raw, far], 0)]
     for stage in reversed(range(core)):
-        far = swap(near, orders, stage)
-        others = [swap(power, orders, stage)]
-        if stage == core - 1:
-            for shift in range(1, shards):
-                others += [across(power, orders, None, shift, shards), across(power, orders, stage, shift, shards)]
-        far, others = lax.optimization_barrier((far, others))
-        power = tree_sum([power] + others)
-        if stage > 0:
-            near = jnp.concatenate([near, far], 0)
-    pieces = [near, far, swap(near, orders, core), swap(far, orders, core)]
-    powers = [power, swap(power, orders, core)]
+        nears = [jnp.concatenate(values, 0) if len(values) > 1 else values[0] for values in (nears, fars) if values]
+        fars = []
+        for value in nears:
+            fars.append(swap(value, orders, stage))
+    tiles = jnp.concatenate([value.reshape(-1, raw.shape[0], block_len)[:, -TILE:] for value in nears], 0)
+    tiles = jnp.stack([
+        jnp.concatenate([across(tiles, orders, turn, shift, shards) for turn in (None, 0)], 0)
+        for shift in range(1, shards)])
+    own = nears + fars
+    other = [swap(value, orders, core) for value in own]
     new_weights, scales, new_momentum, avg_now, sq_now = weights_update(
-        weights, pieces, powers, count_all, offsets, owners, columns, (new_momentum, avg_now, sq_now), orders, width)
+        weights, own, other, tiles, count_all, offsets, owners, columns, (new_momentum, avg_now, sq_now), orders, band_rows, width)
     return (new_weights, new_momentum[None], avg_now.reshape(exp_avg.shape), sq_now.reshape(exp_sq.shape), scales)
 
 

time: 62.6 us -> 58.8 us (0.939)
  starting transfers between devices: 22.8 us -> 18 us
  waiting for transfers between devices: 23.6 us -> 24.3 us
    ppermute x16 -> x17, starting transfers between devices: 18.4 us -> 14.1 us  [swap(): return lax.ppermute(value, 'wide', pairs)]
    ppermute x16 -> x17, waiting for transfers between devices: 23.5 us -> 24 us  [swap(): return lax.ppermute(value, 'wide', pairs)]
  transfers between devices with their start and end apart: 18 -> 19, of which waited for: 10 -> 10; matrix products, arithmetic and copies ran while one was open for 0% -> 0% of each run, Pallas kernels for 5% -> 5%
where the time goes in v1:
time: 58.8 us; the launch traced here: 58.7 us
  waiting for transfers between devices  24.3 us (41%)
  starting transfers between devices  18 us (31%)
  Pallas kernels  15.1 us (26%)
  between operations  0.83 us (1%)
    ppermute x17, waiting for transfers between devices, swap(): return lax.ppermute(value, 'wide', pairs)  24 us
    ppermute x17, starting transfers between devices, swap(): return lax.ppermute(value, 'wide', pairs)  14.1 us
    pallas_call x1, Pallas kernels, bands(): pl.pallas_call(kernel, in_specs=[HBM] * 6, out_specs=[VMEM] * 5, out_shap...  6.51 us
    pallas_call x1, Pallas kernels, weights_update(): pl.pallas_call(kernel, in_specs=[SMEM, SMEM] + [VMEM] * (3 + 2 * pieces +...  5.37 us
    ppermute x2, starting transfers between devices, across(): return lax.ppermute(value, ('wide', 'shard'), pairs)  3.88 us
    pallas_call x1, Pallas kernels, momentum_update(): pl.pallas_call(kernel, in_specs=[SMEM] + [VMEM] * 4, out_specs=VMEM, out_...  3.04 us
  transfers between devices with their start and end apart: 19, of which 10 were waited for; matrix products, arithmetic and copies ran while one was open for 0% of the time, Pallas kernels for 5%

profile of v1, /device:TPU:0, one launch (start us, length us, event | category | flops | bytes accessed | tf_op | source)
XLA Modules:
  0.0 58.7 jit_solution(17751579761080803292)
XLA Ops:
  0.6 6.5 %bands.1 = (bf16[128,8192]{1,0:T(8,128)(2,1)S(1)}, bf16[2,128,8192]{2,1,0:T(8,128)(2,1)S(1)}, f32[2048,128]{1,0:T(8,128)S(1)}, f32[64,32,128]{2,1,0:T(8,128)S(1)}, bf16[64,32,128]{2,1,0:T(8,128)(2,1)S(1)}) custom-call(s32[1,64]{1,0:T(1,128)} %offsets_ref.3, s32[1,64]{1,0:T(1,128)} %owners_ref.1, bf16[128,8192]{1,0:T(8,128)(2,1)} %bitcast.16, ...), custom_call_target="tpu_custom_call" | custom-call | tf_op jit(solution)/shard_map/bands/pallas_call | solution.py:189
  7.2 0.6 collective-permute-start
  7.7 1.5 %collective-permute-done = bf16[64,32,128]{2,1,0:T(8,128)(2,1)S(1)} collective-permute-done((bf16[64,32,128]{2,1,0:T(8,128)(2,1)S(1)}, bf16[64,32,128]{2,1,0:T(8,128)(2,1)S(1)}, u32[]{:S(2)}, u32[]{:S(2)}) %collective-permute-start) | collective-permute-done | bytes 524320 | tf_op jit(solution)/shard_map/ppermute | solution.py:424
  9.3 0.2 fusion.1
  9.5 0.0 copy-start.3
  9.5 0.0 copy-start
  9.5 2.9 %collective-permute-start.2 = (bf16[16,32,128]{2,1,0:T(8,128)(2,1)S(1)}, bf16[16,32,128]{2,1,0:T(8,128)(2,1)S(1)}, u32[]{:S(2)}, u32[]{:S(2)}) collective-permute-start(bf16[16,32,128]{2,1,0:T(8,128)(2,1)S(1)} %get-tuple-element.39), channel_id=1, source_target_pairs={{0,4},{2,10},{4,0},{6,14},{8,12},{10,2},{12,8},{14,6},{16,20},{18,... | collective-permute-start | bytes 393224 | tf_op jit(solution)/shard_map/ppermute | solution.py:424
  12.5 0.1 collective-permute-start.1
  12.6 2.9 %collective-permute-done.2 = bf16[16,32,128]{2,1,0:T(8,128)(2,1)S(1)} collective-permute-done((bf16[16,32,128]{2,1,0:T(8,128)(2,1)S(1)}, bf16[16,32,128]{2,1,0:T(8,128)(2,1)S(1)}, u32[]{:S(2)}, u32[]{:S(2)}) %collective-permute-start.2) | collective-permute-done | bytes 131104 | tf_op jit(solution)/shard_map/ppermute | solution.py:424
  15.5 2.1 %collective-permute-start.3 = (bf16[8,32,128]{2,1,0:T(8,128)(2,1)S(1)}, bf16[8,32,128]{2,1,0:T(8,128)(2,1)S(1)}, u32[]{:S(2)}, u32[]{:S(2)}) collective-permute-start(bf16[8,32,128]{2,1,0:T(8,128)(2,1)S(1)} %get-tuple-element.43), channel_id=1, source_target_pairs={{0,8},{2,6},{4,12},{6,2},{8,0},{10,14},{12,4},{14,10},{16,24},{18,... | collective-permute-start | bytes 196616 | tf_op jit(solution)/shard_map/ppermute | solution.py:424
  17.6 0.1 collective-permute-start.4
  17.8 4.1 %collective-permute-done.4 = bf16[8,32,128]{2,1,0:T(8,128)(2,1)S(1)} collective-permute-done((bf16[8,32,128]{2,1,0:T(8,128)(2,1)S(1)}, bf16[8,32,128]{2,1,0:T(8,128)(2,1)S(1)}, u32[]{:S(2)}, u32[]{:S(2)}) %collective-permute-start.4) | collective-permute-done | bytes 65568 | tf_op jit(solution)/shard_map/ppermute | solution.py:424
  21.9 2.7 %collective-permute-start.5 = (bf16[8,32,128]{2,1,0:T(8,128)(2,1)S(1)}, bf16[8,32,128]{2,1,0:T(8,128)(2,1)S(1)}, u32[]{:S(2)}, u32[]{:S(2)}) collective-permute-start(bf16[8,32,128]{2,1,0:T(8,128)(2,1)S(1)} %slice_add_fusion.2), channel_id=1, source_target_pairs={{0,16},{2,18},{4,20},{6,22},{8,24},{10,26},{12,28},{14,30},{16,0},... | collective-permute-start | bytes 196616 | tf_op jit(solution)/shard_map/ppermute | solution.py:424
  24.6 3.3 %collective-permute-done.5 = bf16[8,32,128]{2,1,0:T(8,128)(2,1)S(1)} collective-permute-done((bf16[8,32,128]{2,1,0:T(8,128)(2,1)S(1)}, bf16[8,32,128]{2,1,0:T(8,128)(2,1)S(1)}, u32[]{:S(2)}, u32[]{:S(2)}) %collective-permute-start.5) | collective-permute-done | bytes 65568 | tf_op jit(solution)/shard_map/ppermute | solution.py:424
  27.9 0.1 collective-permute-start.6
  28.0 1.2 %collective-permute-done.6.got_ref = f32[4,32,128]{2,1,0:T(8,128)S(1)} collective-permute-done((f32[4,32,128]{2,1,0:T(8,128)S(1)}, f32[4,32,128]{2,1,0:T(8,128)S(1)}, u32[]{:S(2)}, u32[]{:S(2)}) %collective-permute-start.6) | collective-permute-done | bytes 65568 | tf_op jit(solution)/shard_map/ppermute | solution.py:424
  29.2 0.1 adam.1
  29.4 0.2 collective-permute-start.7
  29.6 1.0 %collective-permute-done.7 = bf16[144,128]{1,0:T(8,128)(2,1)S(1)} collective-permute-done((bf16[144,128]{1,0:T(8,128)(2,1)S(1)}, bf16[144,128]{1,0:T(8,128)(2,1)S(1)}, u32[]{:S(2)}, u32[]{:S(2)}) %collective-permute-start.7) | collective-permute-done | bytes 36896 | tf_op jit(solution)/shard_map/ppermute | solution.py:424
  30.6 2.0 %collective-permute-start.8 = (bf16[288,128]{1,0:T(8,128)(2,1)S(1)}, bf16[288,128]{1,0:T(8,128)(2,1)S(1)}, u32[]{:S(2)}, u32[]{:S(2)}) collective-permute-start(bf16[288,128]{1,0:T(8,128)(2,1)S(1)} %get-tuple-element.46), channel_id=1, source_target_pairs={{0,16},{2,18},{4,20},{6,22},{8,24},{10,26},{12,28},{14,30},{16,0},... | collective-permute-start | bytes 221192 | tf_op jit(solution)/shard_map/ppermute | solution.py:424
  32.6 0.7 %collective-permute-start.9 = (bf16[288,128]{1,0:T(8,128)(2,1)S(1)}, bf16[288,128]{1,0:T(8,128)(2,1)S(1)}, u32[]{:S(2)}, u32[]{:S(2)}) collective-permute-start(bf16[288,128]{1,0:T(8,128)(2,1)S(1)} %get-tuple-element.46), channel_id=1, source_target_pairs={{0,8},{2,6},{4,12},{6,2},{8,0},{10,14},{12,4},{14,10},{16,24},{18,... | collective-permute-start | bytes 221192 | tf_op jit(solution)/shard_map/ppermute | solution.py:424
  33.3 3.9 %collective-permute-done.8 = bf16[288,128]{1,0:T(8,128)(2,1)S(1)} collective-permute-done((bf16[288,128]{1,0:T(8,128)(2,1)S(1)}, bf16[288,128]{1,0:T(8,128)(2,1)S(1)}, u32[]{:S(2)}, u32[]{:S(2)}) %collective-permute-start.8) | collective-permute-done | bytes 73760 | tf_op jit(solution)/shard_map/ppermute | solution.py:424
  37.2 1.6 %collective-permute-start.13 = (bf16[576,128]{1,0:T(8,128)(2,1)S(1)}, bf16[576,128]{1,0:T(8,128)(2,1)S(1)}, u32[]{:S(2)}, u32[]{:S(2)}) collective-permute-start(bf16[576,128]{1,0:T(8,128)(2,1)S(1)} %constant_dynamic-update-slice_fusion.2.refs_0_), channel_id=1, source_target_pairs={{0,4},{2,10},{4,0},{6,14},{8,12},{10,2},{12,8},{14,6},{16,20},{18,... | collective-permute-start | bytes 442376 | tf_op jit(solution)/shard_map/ppermute | solution.py:424
  38.8 4.3 %collective-permute-done.10 = bf16[288,128]{1,0:T(8,128)(2,1)S(1)} collective-permute-done((bf16[288,128]{1,0:T(8,128)(2,1)S(1)}, bf16[288,128]{1,0:T(8,128)(2,1)S(1)}, u32[]{:S(2)}, u32[]{:S(2)}) %collective-permute-start.10) | collective-permute-done | bytes 73760 | tf_op jit(solution)/shard_map/ppermute | solution.py:424
  43.1 0.6 %collective-permute-start.14 = (bf16[576,128]{1,0:T(8,128)(2,1)S(1)}, bf16[576,128]{1,0:T(8,128)(2,1)S(1)}, u32[]{:S(2)}, u32[]{:S(2)}) collective-permute-start(bf16[576,128]{1,0:T(8,128)(2,1)S(1)} %constant_dynamic-update-slice_fusion.5.refs_1_), channel_id=1, source_target_pairs={{0,4},{2,10},{4,0},{6,14},{8,12},{10,2},{12,8},{14,6},{16,20},{18,... | collective-permute-start | bytes 442376 | tf_op jit(solution)/shard_map/ppermute | solution.py:424
  43.8 2.4 %collective-permute-start.12 = (bf16[8,16,128]{2,1,0:T(8,128)(2,1)S(1)}, bf16[8,16,128]{2,1,0:T(8,128)(2,1)S(1)}, u32[]{:S(2)}, u32[]{:S(2)}) collective-permute-start(bf16[8,16,128]{2,1,0:T(8,128)(2,1)S(1)} %pad_maximum_fusion), channel_id=1, source_target_pairs={{0,5},{1,4},{2,11},{3,10},{4,1},{5,0},{6,15},{7,14},{8,13},{9,12},... | collective-permute-start | bytes 98312 | tf_op jit(solution)/shard_map/ppermute | solution.py:432
  46.2 0.5 collective-permute-start.16
  46.7 1.6 %collective-permute-done.14.refs_3_ = bf16[576,128]{1,0:T(8,128)(2,1)S(1)} collective-permute-done((bf16[576,128]{1,0:T(8,128)(2,1)S(1)}, bf16[576,128]{1,0:T(8,128)(2,1)S(1)}, u32[]{:S(2)}, u32[]{:S(2)}) %collective-permute-start.14) | collective-permute-done | bytes 147488 | tf_op jit(solution)/shard_map/ppermute | solution.py:424
  48.3 0.3 collective-permute-done.12
  48.7 1.5 %collective-permute-start.11 = (bf16[8,16,128]{2,1,0:T(8,128)(2,1)S(1)}, bf16[8,16,128]{2,1,0:T(8,128)(2,1)S(1)}, u32[]{:S(2)}, u32[]{:S(2)}) collective-permute-start(bf16[8,16,128]{2,1,0:T(8,128)(2,1)S(1)} %pad_maximum_fusion), channel_id=1, source_target_pairs={{0,1},{1,0},{2,3},{3,2},{4,5},{5,4},{6,7},{7,6},{8,9},{9,8},{10,11... | collective-permute-start | bytes 98312 | tf_op jit(solution)/shard_map/ppermute | solution.py:432
  50.1 3.0 %momentum_update.1.refs_8_ = bf16[128,8192]{1,0:T(8,128)(2,1)S(1)} custom-call(s32[1,64]{1,0:T(1,128)S(1)} %copy-done.4, bf16[128,8192]{1,0:T(8,128)(2,1)S(1)} %get-tuple-element.27.momentum_ref, bf16[2,128,8192]{2,1,0:T(8,128)(2,1)S(1)} %get-tuple-element.28.grads_ref, f32[2048,128]{1,0:T(8,128)S(1)} %get-tuple-element.29.taken_ref, ...), custom_call_target="tpu_custom_call" | custom-call | tf_op jit(solution)/shard_map/momentum_update/pallas_call | solution.py:264
  53.3 5.4 %weights_update.1 = (bf16[128,8192]{1,0:T(8,128)(2,1)}, f32[2]{0:T(128)}, bf16[128,8192]{1,0:T(8,128)(2,1)}, f32[4,32,128]{2,1,0:T(8,128)}, f32[4,32,128]{2,1,0:T(8,128)}) custom-call(s32[1,64]{1,0:T(1,128)S(1)} %copy-done.4, s32[1,64]{1,0:T(1,128)S(1)} %copy-done.5, bf16[1,16,16,128]{3,2,1,0:T(8,128)(2,1)S(1)} %maximum_bitcast_fusion.tiles_ref, ...), custom_call_target="tpu_custom_call" | custom-call | tf_op jit(solution)/shard_map/weights_update/pallas_call | solution.py:403
  (39 shorter events, 0.3 us)
Async XLA Ops:
  7.2 2.1 %collective-permute-start = (bf16[64,32,128]{2,1,0:T(8,128)(2,1)S(1)}, bf16[64,32,128]{2,1,0:T(8,128)(2,1)S(1)}, u32[]{:S(2)}, u32[]{:S(2)}) collective-permute-start(bf16[64,32,128]{2,1,0:T(8,128)(2,1)S(1)} %get-tuple-element.22), channel_id=1, source_target_pairs={{0,2},{2,0},{4,6},{6,4},{8,10},{10,8},{12,14},{14,12},{16,18},{18,... | collective-permute-start | bytes 1572872 | tf_op jit(solution)/shard_map/ppermute | solution.py:424
  9.5 19.7 %copy-start.2 = (f32[1,4,32,128]{3,2,1,0:T(8,128)S(1)}, f32[1,4,32,128]{3,2,1,0:T(8,128)}, u32[]{:S(2)}) copy-start(f32[1,4,32,128]{3,2,1,0:T(8,128)} %param.14) | copy-start | bytes 196612
  9.5 19.7 %copy-start.3 = (f32[1,4,32,128]{3,2,1,0:T(8,128)S(1)}, f32[1,4,32,128]{3,2,1,0:T(8,128)}, u32[]{:S(2)}) copy-start(f32[1,4,32,128]{3,2,1,0:T(8,128)} %param.15) | copy-start | bytes 196612
  9.5 40.6 %copy-start = (bf16[3,256,256]{2,1,0:T(8,128)(2,1)S(1)}, bf16[3,256,256]{2,1,0:T(8,128)(2,1)}, u32[]{:S(2)}) copy-start(bf16[3,256,256]{2,1,0:T(8,128)(2,1)} %constant.5.clone.columns_hbm.columns_ref) | copy-start | bytes 1179652
  9.5 40.6 %copy-start.4 = (s32[1,64]{1,0:T(1,128)S(1)}, s32[1,64]{1,0:T(1,128)}, u32[]{:S(2)}) copy-start(s32[1,64]{1,0:T(1,128)} %offsets_ref.3) | copy-start | bytes 772
  9.5 5.9 %collective-permute-start.2 = (bf16[16,32,128]{2,1,0:T(8,128)(2,1)S(1)}, bf16[16,32,128]{2,1,0:T(8,128)(2,1)S(1)}, u32[]{:S(2)}, u32[]{:S(2)}) collective-permute-start(bf16[16,32,128]{2,1,0:T(8,128)(2,1)S(1)} %get-tuple-element.39), channel_id=1, source_target_pairs={{0,4},{2,10},{4,0},{6,14},{8,12},{10,2},{12,8},{14,6},{16,20},{18,... | collective-permute-start | bytes 393224 | tf_op jit(solution)/shard_map/ppermute | solution.py:424
  12.5 5.2 %collective-permute-start.1 = (bf16[16,32,128]{2,1,0:T(8,128)(2,1)S(1)}, bf16[16,32,128]{2,1,0:T(8,128)(2,1)S(1)}, u32[]{:S(2)}, u32[]{:S(2)}) collective-permute-start(bf16[16,32,128]{2,1,0:T(8,128)(2,1)S(1)} %get-tuple-element.40), channel_id=1, source_target_pairs={{0,4},{2,10},{4,0},{6,14},{8,12},{10,2},{12,8},{14,6},{16,20},{18,... | collective-permute-start | bytes 393224 | tf_op jit(solution)/shard_map/ppermute | solution.py:424
  15.5 9.1 %collective-permute-start.3 = (bf16[8,32,128]{2,1,0:T(8,128)(2,1)S(1)}, bf16[8,32,128]{2,1,0:T(8,128)(2,1)S(1)}, u32[]{:S(2)}, u32[]{:S(2)}) collective-permute-start(bf16[8,32,128]{2,1,0:T(8,128)(2,1)S(1)} %get-tuple-element.43), channel_id=1, source_target_pairs={{0,8},{2,6},{4,12},{6,2},{8,0},{10,14},{12,4},{14,10},{16,24},{18,... | collective-permute-start | bytes 196616 | tf_op jit(solution)/shard_map/ppermute | solution.py:424
  17.6 4.3 %collective-permute-start.4 = (bf16[8,32,128]{2,1,0:T(8,128)(2,1)S(1)}, bf16[8,32,128]{2,1,0:T(8,128)(2,1)S(1)}, u32[]{:S(2)}, u32[]{:S(2)}) collective-permute-start(bf16[8,32,128]{2,1,0:T(8,128)(2,1)S(1)} %get-tuple-element.44), channel_id=1, source_target_pairs={{0,8},{2,6},{4,12},{6,2},{8,0},{10,14},{12,4},{14,10},{16,24},{18,... | collective-permute-start | bytes 196616 | tf_op jit(solution)/shard_map/ppermute | solution.py:424
  21.9 5.9 %collective-permute-start.5 = (bf16[8,32,128]{2,1,0:T(8,128)(2,1)S(1)}, bf16[8,32,128]{2,1,0:T(8,128)(2,1)S(1)}, u32[]{:S(2)}, u32[]{:S(2)}) collective-permute-start(bf16[8,32,128]{2,1,0:T(8,128)(2,1)S(1)} %slice_add_fusion.2), channel_id=1, source_target_pairs={{0,16},{2,18},{4,20},{6,22},{8,24},{10,26},{12,28},{14,30},{16,0},... | collective-permute-start | bytes 196616 | tf_op jit(solution)/shard_map/ppermute | solution.py:424
  27.9 1.3 %collective-permute-start.6 = (f32[4,32,128]{2,1,0:T(8,128)S(1)}, f32[4,32,128]{2,1,0:T(8,128)S(1)}, u32[]{:S(2)}, u32[]{:S(2)}) collective-permute-start(f32[4,32,128]{2,1,0:T(8,128)S(1)} %get-tuple-element.41), channel_id=1, source_target_pairs={{0,2},{2,0},{4,6},{6,4},{8,10},{10,8},{12,14},{14,12},{16,18},{18,... | collective-permute-start | bytes 196616 | tf_op jit(solution)/shard_map/ppermute | solution.py:424
  29.4 1.3 %collective-permute-start.7 = (bf16[144,128]{1,0:T(8,128)(2,1)S(1)}, bf16[144,128]{1,0:T(8,128)(2,1)S(1)}, u32[]{:S(2)}, u32[]{:S(2)}) collective-permute-start(bf16[144,128]{1,0:T(8,128)(2,1)S(1)} %get-tuple-element.26), channel_id=1, source_target_pairs={{0,2},{2,0},{4,6},{6,4},{8,10},{10,8},{12,14},{14,12},{16,18},{18,... | collective-permute-start | bytes 110600 | tf_op jit(solution)/shard_map/ppermute | solution.py:424
  30.6 6.5 %collective-permute-start.8 = (bf16[288,128]{1,0:T(8,128)(2,1)S(1)}, bf16[288,128]{1,0:T(8,128)(2,1)S(1)}, u32[]{:S(2)}, u32[]{:S(2)}) collective-permute-start(bf16[288,128]{1,0:T(8,128)(2,1)S(1)} %get-tuple-element.46), channel_id=1, source_target_pairs={{0,16},{2,18},{4,20},{6,22},{8,24},{10,26},{12,28},{14,30},{16,0},... | collective-permute-start | bytes 221192 | tf_op jit(solution)/shard_map/ppermute | solution.py:424
  32.6 6.2 %collective-permute-start.9 = (bf16[288,128]{1,0:T(8,128)(2,1)S(1)}, bf16[288,128]{1,0:T(8,128)(2,1)S(1)}, u32[]{:S(2)}, u32[]{:S(2)}) collective-permute-start(bf16[288,128]{1,0:T(8,128)(2,1)S(1)} %get-tuple-element.46), channel_id=1, source_target_pairs={{0,8},{2,6},{4,12},{6,2},{8,0},{10,14},{12,4},{14,10},{16,24},{18,... | collective-permute-start | bytes 221192 | tf_op jit(solution)/shard_map/ppermute | solution.py:424
  37.2 9.5 %collective-permute-start.13 = (bf16[576,128]{1,0:T(8,128)(2,1)S(1)}, bf16[576,128]{1,0:T(8,128)(2,1)S(1)}, u32[]{:S(2)}, u32[]{:S(2)}) collective-permute-start(bf16[576,128]{1,0:T(8,128)(2,1)S(1)} %constant_dynamic-update-slice_fusion.2.refs_0_), channel_id=1, source_target_pairs={{0,4},{2,10},{4,0},{6,14},{8,12},{10,2},{12,8},{14,6},{16,20},{18,... | collective-permute-start | bytes 442376 | tf_op jit(solution)/shard_map/ppermute | solution.py:424
  38.7 4.4 %collective-permute-start.10 = (bf16[288,128]{1,0:T(8,128)(2,1)S(1)}, bf16[288,128]{1,0:T(8,128)(2,1)S(1)}, u32[]{:S(2)}, u32[]{:S(2)}) collective-permute-start(bf16[288,128]{1,0:T(8,128)(2,1)S(1)} %collective-permute-done.8), channel_id=1, source_target_pairs={{0,8},{2,6},{4,12},{6,2},{8,0},{10,14},{12,4},{14,10},{16,24},{18,... | collective-permute-start | bytes 221192 | tf_op jit(solution)/shard_map/ppermute | solution.py:424
  43.1 5.2 %collective-permute-start.14 = (bf16[576,128]{1,0:T(8,128)(2,1)S(1)}, bf16[576,128]{1,0:T(8,128)(2,1)S(1)}, u32[]{:S(2)}, u32[]{:S(2)}) collective-permute-start(bf16[576,128]{1,0:T(8,128)(2,1)S(1)} %constant_dynamic-update-slice_fusion.5.refs_1_), channel_id=1, source_target_pairs={{0,4},{2,10},{4,0},{6,14},{8,12},{10,2},{12,8},{14,6},{16,20},{18,... | collective-permute-start | bytes 442376 | tf_op jit(solution)/shard_map/ppermute | solution.py:424
  43.8 4.9 %collective-permute-start.12 = (bf16[8,16,128]{2,1,0:T(8,128)(2,1)S(1)}, bf16[8,16,128]{2,1,0:T(8,128)(2,1)S(1)}, u32[]{:S(2)}, u32[]{:S(2)}) collective-permute-start(bf16[8,16,128]{2,1,0:T(8,128)(2,1)S(1)} %pad_maximum_fusion), channel_id=1, source_target_pairs={{0,5},{1,4},{2,11},{3,10},{4,1},{5,0},{6,15},{7,14},{8,13},{9,12},... | collective-permute-start | bytes 98312 | tf_op jit(solution)/shard_map/ppermute | solution.py:432
  46.2 7.0 %collective-permute-start.15 = (bf16[576,128]{1,0:T(8,128)(2,1)S(1)}, bf16[576,128]{1,0:T(8,128)(2,1)S(1)}, u32[]{:S(2)}, u32[]{:S(2)}) collective-permute-start(bf16[576,128]{1,0:T(8,128)(2,1)S(1)} %constant_dynamic-update-slice_fusion.2.refs_0_), channel_id=1, source_target_pairs={{0,2},{2,0},{4,6},{6,4},{8,10},{10,8},{12,14},{14,12},{16,18},{18,... | collective-permute-start | bytes 442376 | tf_op jit(solution)/shard_map/ppermute | solution.py:424
  46.2 7.1 %collective-permute-start.16 = (bf16[576,128]{1,0:T(8,128)(2,1)S(1)}, bf16[576,128]{1,0:T(8,128)(2,1)S(1)}, u32[]{:S(2)}, u32[]{:S(2)}) collective-permute-start(bf16[576,128]{1,0:T(8,128)(2,1)S(1)} %constant_dynamic-update-slice_fusion.5.refs_1_), channel_id=1, source_target_pairs={{0,2},{2,0},{4,6},{6,4},{8,10},{10,8},{12,14},{14,12},{16,18},{18,... | collective-permute-start | bytes 442376 | tf_op jit(solution)/shard_map/ppermute | solution.py:424
  46.7 6.6 %collective-permute-start.17 = (bf16[576,128]{1,0:T(8,128)(2,1)S(1)}, bf16[576,128]{1,0:T(8,128)(2,1)S(1)}, u32[]{:S(2)}, u32[]{:S(2)}) collective-permute-start(bf16[576,128]{1,0:T(8,128)(2,1)S(1)} %collective-permute-done.13.refs_2_), channel_id=1, source_target_pairs={{0,2},{2,0},{4,6},{6,4},{8,10},{10,8},{12,14},{14,12},{16,18},{18,... | collective-permute-start | bytes 442376 | tf_op jit(solution)/shard_map/ppermute | solution.py:424
  48.3 4.9 %collective-permute-start.18 = (bf16[576,128]{1,0:T(8,128)(2,1)S(1)}, bf16[576,128]{1,0:T(8,128)(2,1)S(1)}, u32[]{:S(2)}, u32[]{:S(2)}) collective-permute-start(bf16[576,128]{1,0:T(8,128)(2,1)S(1)} %collective-permute-done.14.refs_3_), channel_id=1, source_target_pairs={{0,2},{2,0},{4,6},{6,4},{8,10},{10,8},{12,14},{14,12},{16,18},{18,... | collective-permute-start | bytes 442376 | tf_op jit(solution)/shard_map/ppermute | solution.py:424
  48.7 4.5 %collective-permute-start.11 = (bf16[8,16,128]{2,1,0:T(8,128)(2,1)S(1)}, bf16[8,16,128]{2,1,0:T(8,128)(2,1)S(1)}, u32[]{:S(2)}, u32[]{:S(2)}) collective-permute-start(bf16[8,16,128]{2,1,0:T(8,128)(2,1)S(1)} %pad_maximum_fusion), channel_id=1, source_target_pairs={{0,1},{1,0},{2,3},{3,2},{4,5},{5,4},{6,7},{7,6},{8,9},{9,8},{10,11... | collective-permute-start | bytes 98312 | tf_op jit(solution)/shard_map/ppermute | solution.py:432
  50.1 3.1 %copy-start.1 = (bf16[128,8192]{1,0:T(8,128)(2,1)S(1)}, bf16[128,8192]{1,0:T(8,128)(2,1)}, u32[]{:S(2)}) copy-start(bf16[128,8192]{1,0:T(8,128)(2,1)} %weights_ref.1) | copy-start | bytes 6291460
  50.1 3.1 %copy-start.5 = (s32[1,64]{1,0:T(1,128)S(1)}, s32[1,64]{1,0:T(1,128)}, u32[]{:S(2)}) copy-start(s32[1,64]{1,0:T(1,128)} %owners_ref.1) | copy-start | bytes 772

commit v2 on v1

--- a/solution.py
+++ b/solution.py
@@ -272,46 +272,47 @@
     )(offsets, *map(near_memory, (momentum, grads, taken, columns)))
 
 
-def adam(mine, got, exp_avg, exp_sq, replicas):
+def adam(mine, got, exp_avg, exp_sq, others, replicas):
     flat = exp_avg.shape
+    count = flat[0]
     block_len = flat[-1]
     rows = flat[0] * flat[1]
 
-    def kernel(mine_ref, got_ref, avg_ref, sq_ref, avg_out, sq_out, raw_keep, raw_send):
+    def kernel(mine_ref, got_ref, avg_ref, sq_ref, others_ref, avg_out, sq_out, raw_out):
         first_role = (lax.axis_index("wide") & 1) == 0
-        own = mine_ref[...]
-        other = got_ref[...]
-        avg = avg_ref[...]
-        sq = sq_ref[...]
         row = lax.broadcasted_iota(jnp.int32, (TILE, block_len), 0)
+        powers = []
+        for core, (avg, sq) in enumerate(((avg_ref[...], sq_ref[...]), (others_ref[0], others_ref[1]))):
+            own = mine_ref[core * count:(core + 1) * count]
+            other = got_ref[(1 - core) * count:(2 - core) * count]
+            raws = []
+            for total in (jnp.where(first_role, own, other), jnp.where(first_role, other, own)):
+                mean_band = total / replicas
+                avg = beta_one * avg + (1.0 - beta_one) * mean_band
+                sq = beta_two * sq + (1.0 - beta_two) * mean_band * mean_band
+                raws.append((avg / (jnp.sqrt(sq) + adam_eps)).reshape(rows, block_len))
+            if core == 0:
+                avg_out[...] = avg
+                sq_out[...] = sq
+            raw_out[core * rows:(core + 1) * rows, :] = jnp.where(first_role, raws[0], raws[1]).astype(jnp.bfloat16)
+            powers.append([jnp.sum(raw * raw, axis=0, keepdims=True) for raw in raws])
         tile = jnp.zeros((TILE, block_len), jnp.float32)
-        raws = []
-        for step_index, total in enumerate((jnp.where(first_role, own, other), jnp.where(first_role, other, own))):
-            mean_band = total / replicas
-            avg = beta_one * avg + (1.0 - beta_one) * mean_band
-            sq = beta_two * sq + (1.0 - beta_two) * mean_band * mean_band
-            raw = avg / (jnp.sqrt(sq) + adam_eps)
-            raws.append(raw.reshape(rows, block_len))
-            rest = jnp.sum(raws[-1] * raws[-1], axis=0, keepdims=True)
+        for step_index in range(STEPS):
+            rest = powers[0][step_index] + powers[1][step_index]
             for part in range(3):
                 piece = rest.astype(jnp.bfloat16).astype(jnp.float32)
                 tile = jnp.where(row == STEPS * part + step_index, piece, tile)
                 rest = rest - piece
-        avg_out[...] = avg
-        sq_out[...] = sq
-        raw_keep[:rows, :] = jnp.where(first_role, raws[0], raws[1]).astype(jnp.bfloat16)
-        raw_send[:rows, :] = jnp.where(first_role, raws[1], raws[0]).astype(jnp.bfloat16)
-        raw_keep[rows:, :] = tile.astype(jnp.bfloat16)
-        raw_send[rows:, :] = tile.astype(jnp.bfloat16)
+        raw_out[2 * rows:, :] = tile.astype(jnp.bfloat16)
 
     return pl.pallas_call(
         kernel,
-        in_specs=[VMEM] * 4,
-        out_specs=[VMEM] * 4,
-        out_shape=[pltpu.VMEM(flat, jnp.float32)] * 2 + [pltpu.VMEM((rows + TILE, block_len), jnp.bfloat16)] * 2,
+        in_specs=[VMEM] * 5,
+        out_specs=[VMEM] * 3,
+        out_shape=[pltpu.VMEM(flat, jnp.float32)] * 2 + [pltpu.VMEM((2 * rows + TILE, block_len), jnp.bfloat16)],
         compiler_params=SMALL,
         name="adam",
-    )(*map(near_memory, (mine, got, exp_avg, exp_sq)))
+    )(*map(near_memory, (mine, got, exp_avg, exp_sq, others)))
 
 
 def weights_update(weights, own, other, tiles, count_all, offsets, owners, columns, ready, orders, band_rows, width):
@@ -319,7 +320,7 @@
     block_len = columns.shape[-1] // 2
     size = own[0].shape[0]
     pieces = len(own)
-    stride = size * pieces >> len(orders[0])
+    stride = 2 * size * pieces >> len(orders[0])
     shift = (size // stride).bit_length() - 1
     shards = tiles.shape[0] + 1
     owned = col_blocks >> len(orders[0])
@@ -347,8 +348,8 @@
         scales = []
         rows = [[ref[begin + stride - TILE:begin + stride, :] for ref in piece_refs[0] for begin in range(0, size, stride)]]
         for shard in range(shards - 1):
-            rows.append([tiles_ref[shard, group] for group in range(1 << len(orders[0]))])
-        tile = tree_sum([axis_sum([value.astype(jnp.float32) for value in values], orders, first_role) for values in rows])
+            rows.append([tiles_ref[shard, group] for group in range(1 << len(orders[0]) - 1)])
+        tile = tree_sum([axis_sum([value.astype(jnp.float32) for value in values], [order[:-1] for order in orders], first_role) for values in rows])
         parity = lax.broadcasted_iota(jnp.int32, tile.shape, 0) & 1
         for step_index in range(STEPS):
             power = jnp.sum(jnp.where(parity == step_index, tile, 0.0), keepdims=True)
@@ -376,8 +377,10 @@
                 total = jnp.zeros((band_rows, block_len), jnp.float32)
                 for number in range(STEPS):
                     group = groups_ref[role ^ number, owner ^ device ^ number]
-                    which = group >> shift
-                    rows = pl.ds(pl.multiple_of((group & ((1 << shift) - 1)) * stride + within, TILE), band_rows)
+                    chip = group >> 1
+                    which = chip >> shift
+                    begin = (chip & ((1 << shift) - 1)) * stride + (group & 1) * (row_blocks * owned * band_rows) + within
+                    rows = pl.ds(pl.multiple_of(begin, TILE), band_rows)
                     raw = piece_refs[number][0][rows, :]
                     for piece in range(1, pieces):
                         raw = jnp.where(which == piece, piece_refs[number][piece][rows, :], raw)
@@ -438,7 +441,7 @@
         entries = {}
         for place, value in enumerate(values):
             digits = [place >> (len(order) - 1 - position) & 1 for position in range(len(order))]
-            entries[sum(digit << bit for digit, bit in zip(digits, order))] = value
+            entries[sum(digit << bit - 1 for digit, bit in zip(digits, order))] = value
         current = [entries[index] for index in range(len(values))]
         sums.append(tree_sum(current))
     return jnp.where(first_role, *sums)
@@ -465,28 +468,30 @@
         orders[1][:2] = orders[1][1::-1]
     core = bits - 1
     near_momentum, near_grads, taken, kept, sent = bands(
-        momentum[0], grads[:, 0], offsets, owners, picks, columns, band_rows, orders, width)
+        momentum[0], grads[:, 0], offsets, owners, picks, columns, band_rows, orders, 2 * width)
     new_momentum = momentum_update(near_momentum, near_grads, taken, offsets, columns, band_rows, width)
-    got = swap(sent, orders, core)
-    kept = kept + got.astype(jnp.float32)
     middle = kept.shape[0] // 2
-    keep, send = kept[:middle], kept[middle:]
+    high = swap(sent[middle:], orders, core)
+    low = swap(sent[:middle], orders, core)
+    send = kept[middle:] + high.astype(jnp.float32)
+    low, _ = lax.optimization_barrier((low, send))
+    keep = kept[:middle] + low.astype(jnp.float32)
     for stage in range(core):
         middle = send.shape[0] // 2
         if stage == core - 1:
             keep = keep + swap(send.astype(jnp.bfloat16), orders, stage).astype(jnp.float32)
-            keep, send = keep[:middle], keep[middle:]
             break
         high = swap(send[middle:].astype(jnp.bfloat16), orders, stage)
         low = swap(send[:middle].astype(jnp.bfloat16), orders, stage)
         send = keep[middle:] + high.astype(jnp.float32)
         low, _ = lax.optimization_barrier((low, send))
         keep = keep[:middle] + low.astype(jnp.float32)
-    got = swap(send, orders, core)
     flat = (row_blocks * owned, band_rows, block_len)
-    avg_now, sq_now, raw, raw_other = adam(keep, got, exp_avg.reshape(flat), exp_sq.reshape(flat), replicas)
-    far = swap(raw_other, orders, core)
-    nears, fars = [], [jnp.concatenate([raw, far], 0)]
+    exp_avg_now, exp_sq_now = exp_avg.reshape(flat), exp_sq.reshape(flat)
+    others = swap(jnp.stack([exp_avg_now, exp_sq_now]), orders, core)
+    got = swap(keep, orders, core)
+    avg_now, sq_now, raw = adam(keep, got, exp_avg_now, exp_sq_now, others, replicas)
+    nears, fars = [], [raw]
     for stage in reversed(range(core)):
         nears = [jnp.concatenate(values, 0) if len(values) > 1 else values[0] for values in (nears, fars) if values]
         fars = []

time: 58.8 us -> 58.1 us (0.988)
  waiting for transfers between devices: 24.3 us -> 22.2 us
  starting transfers between devices: 18 us -> 19.8 us
    ppermute x17 -> x18, waiting for transfers between devices: 24 us -> 21 us  [swap(): return lax.ppermute(value, 'wide', pairs)]
    ppermute x17 -> x18, starting transfers between devices: 14.1 us -> 16.9 us  [swap(): return lax.ppermute(value, 'wide', pairs)]
    ppermute x2, starting transfers between devices: 3.88 us -> 2.94 us  [across(): return lax.ppermute(value, ('wide', 'shard'), pairs)]
    ppermute x2, waiting for transfers between devices: 0.34 us -> 1.18 us  [across(): return lax.ppermute(value, ('wide', 'shard'), pairs)]
  transfers between devices with their start and end apart: 19 -> 20, of which waited for: 10 -> 10; matrix products, arithmetic and copies ran while one was open for 0% -> 1% of each run, Pallas kernels for 5% -> 5%
where the time goes in v2:
time: 58.1 us; the launch traced here: 58 us
  waiting for transfers between devices  22.2 us (38%)
  starting transfers between devices  19.8 us (34%)
  Pallas kernels  14.8 us (25%)
  between operations  0.83 us (1%)
    ppermute x18, waiting for transfers between devices, swap(): return lax.ppermute(value, 'wide', pairs)  21 us
    ppermute x18, starting transfers between devices, swap(): return lax.ppermute(value, 'wide', pairs)  16.9 us
    pallas_call x1, Pallas kernels, bands(): pl.pallas_call(kernel, in_specs=[HBM] * 6, out_specs=[VMEM] * 5, out_shap...  6.02 us
    pallas_call x1, Pallas kernels, weights_update(): pl.pallas_call(kernel, in_specs=[SMEM, SMEM] + [VMEM] * (3 + 2 * pieces +...  5.52 us
    pallas_call x1, Pallas kernels, momentum_update(): pl.pallas_call(kernel, in_specs=[SMEM] + [VMEM] * 4, out_specs=VMEM, out_...  3.06 us
    ppermute x2, starting transfers between devices, across(): return lax.ppermute(value, ('wide', 'shard'), pairs)  2.94 us
    ppermute x2, waiting for transfers between devices, across(): return lax.ppermute(value, ('wide', 'shard'), pairs)  1.18 us
  transfers between devices with their start and end apart: 20, of which 10 were waited for; matrix products, arithmetic and copies ran while one was open for 1% of the time, Pallas kernels for 5%

profile of v2, /device:TPU:0, one launch (start us, length us, event | category | flops | bytes accessed | tf_op | source)
XLA Modules:
  0.0 58.0 jit_solution(14163684040829211917)
XLA Ops:
  0.6 6.0 %bands.1 = (bf16[128,8192]{1,0:T(8,128)(2,1)S(1)}, bf16[2,128,8192]{2,1,0:T(8,128)(2,1)S(1)}, f32[2048,128]{1,0:T(8,128)S(1)}, f32[64,32,128]{2,1,0:T(8,128)S(1)}, bf16[64,32,128]{2,1,0:T(8,128)(2,1)S(1)}) custom-call(s32[1,64]{1,0:T(1,128)} %offsets_ref.3, s32[1,64]{1,0:T(1,128)} %owners_ref.1, bf16[128,8192]{1,0:T(8,128)(2,1)} %bitcast.16, ...), custom_call_target="tpu_custom_call" | custom-call | tf_op jit(solution)/shard_map/bands/pallas_call | solution.py:189
  6.7 0.6 collective-permute-start.1
  7.3 0.1 collective-permute-start
  7.3 1.1 %collective-permute-done.1 = bf16[32,32,128]{2,1,0:T(8,128)(2,1)S(1)} collective-permute-done((bf16[32,32,128]{2,1,0:T(8,128)(2,1)S(1)}, bf16[32,32,128]{2,1,0:T(8,128)(2,1)S(1)}, u32[]{:S(2)}, u32[]{:S(2)}) %collective-permute-start.1) | collective-permute-done | bytes 262176 | tf_op jit(solution)/shard_map/ppermute | solution.py:427
  8.5 2.9 %collective-permute-start.3 = (bf16[16,32,128]{2,1,0:T(8,128)(2,1)S(1)}, bf16[16,32,128]{2,1,0:T(8,128)(2,1)S(1)}, u32[]{:S(2)}, u32[]{:S(2)}) collective-permute-start(bf16[16,32,128]{2,1,0:T(8,128)(2,1)S(1)} %get-tuple-element.39), channel_id=1, source_target_pairs={{0,4},{2,10},{4,0},{6,14},{8,12},{10,2},{12,8},{14,6},{16,20},{18,... | collective-permute-start | bytes 393224 | tf_op jit(solution)/shard_map/ppermute | solution.py:427
  11.5 0.1 collective-permute-start.2
  11.6 0.1 convert_add_fusion
  11.6 2.8 %collective-permute-done.3 = bf16[16,32,128]{2,1,0:T(8,128)(2,1)S(1)} collective-permute-done((bf16[16,32,128]{2,1,0:T(8,128)(2,1)S(1)}, bf16[16,32,128]{2,1,0:T(8,128)(2,1)S(1)}, u32[]{:S(2)}, u32[]{:S(2)}) %collective-permute-start.3) | collective-permute-done | bytes 131104 | tf_op jit(solution)/shard_map/ppermute | solution.py:427
  14.5 2.0 %collective-permute-done.2 = bf16[16,32,128]{2,1,0:T(8,128)(2,1)S(1)} collective-permute-done((bf16[16,32,128]{2,1,0:T(8,128)(2,1)S(1)}, bf16[16,32,128]{2,1,0:T(8,128)(2,1)S(1)}, u32[]{:S(2)}, u32[]{:S(2)}) %collective-permute-start.2) | collective-permute-done | bytes 131104 | tf_op jit(solution)/shard_map/ppermute | solution.py:427
  16.4 1.6 %collective-permute-start.5 = (bf16[8,32,128]{2,1,0:T(8,128)(2,1)S(1)}, bf16[8,32,128]{2,1,0:T(8,128)(2,1)S(1)}, u32[]{:S(2)}, u32[]{:S(2)}) collective-permute-start(bf16[8,32,128]{2,1,0:T(8,128)(2,1)S(1)} %get-tuple-element.42), channel_id=1, source_target_pairs={{0,8},{2,6},{4,12},{6,2},{8,0},{10,14},{12,4},{14,10},{16,24},{18,... | collective-permute-start | bytes 196616 | tf_op jit(solution)/shard_map/ppermute | solution.py:427
  18.0 0.5 collective-permute-start.4
  18.6 2.1 %collective-permute-done.5 = bf16[8,32,128]{2,1,0:T(8,128)(2,1)S(1)} collective-permute-done((bf16[8,32,128]{2,1,0:T(8,128)(2,1)S(1)}, bf16[8,32,128]{2,1,0:T(8,128)(2,1)S(1)}, u32[]{:S(2)}, u32[]{:S(2)}) %collective-permute-start.5) | collective-permute-done | bytes 65568 | tf_op jit(solution)/shard_map/ppermute | solution.py:427
  20.7 2.7 %collective-permute-start.6 = (bf16[8,32,128]{2,1,0:T(8,128)(2,1)S(1)}, bf16[8,32,128]{2,1,0:T(8,128)(2,1)S(1)}, u32[]{:S(2)}, u32[]{:S(2)}) collective-permute-start(bf16[8,32,128]{2,1,0:T(8,128)(2,1)S(1)} %slice_add_fusion.2), channel_id=1, source_target_pairs={{0,16},{2,18},{4,20},{6,22},{8,24},{10,26},{12,28},{14,30},{16,0},... | collective-permute-start | bytes 196616 | tf_op jit(solution)/shard_map/ppermute | solution.py:427
  23.4 0.1 collective-permute-start.8
  23.5 2.5 %collective-permute-done.6 = bf16[8,32,128]{2,1,0:T(8,128)(2,1)S(1)} collective-permute-done((bf16[8,32,128]{2,1,0:T(8,128)(2,1)S(1)}, bf16[8,32,128]{2,1,0:T(8,128)(2,1)S(1)}, u32[]{:S(2)}, u32[]{:S(2)}) %collective-permute-start.6) | collective-permute-done | bytes 65568 | tf_op jit(solution)/shard_map/ppermute | solution.py:427
  26.0 0.1 collective-permute-start.7
  26.1 1.3 %collective-permute-done.7.got_ref = f32[8,32,128]{2,1,0:T(8,128)S(1)} collective-permute-done((f32[8,32,128]{2,1,0:T(8,128)S(1)}, f32[8,32,128]{2,1,0:T(8,128)S(1)}, u32[]{:S(2)}, u32[]{:S(2)}) %collective-permute-start.7) | collective-permute-done | bytes 131104 | tf_op jit(solution)/shard_map/ppermute | solution.py:427
  27.4 0.2 adam.1
  27.6 1.6 %collective-permute-start.10 = (bf16[272,128]{1,0:T(8,128)(2,1)S(1)}, bf16[272,128]{1,0:T(8,128)(2,1)S(1)}, u32[]{:S(2)}, u32[]{:S(2)}) collective-permute-start(bf16[272,128]{1,0:T(8,128)(2,1)S(1)} %get-tuple-element.26), channel_id=1, source_target_pairs={{0,8},{2,6},{4,12},{6,2},{8,0},{10,14},{12,4},{14,10},{16,24},{18,... | collective-permute-start | bytes 208904 | tf_op jit(solution)/shard_map/ppermute | solution.py:427
  29.2 3.2 %collective-permute-start.9 = (bf16[272,128]{1,0:T(8,128)(2,1)S(1)}, bf16[272,128]{1,0:T(8,128)(2,1)S(1)}, u32[]{:S(2)}, u32[]{:S(2)}) collective-permute-start(bf16[272,128]{1,0:T(8,128)(2,1)S(1)} %get-tuple-element.26), channel_id=1, source_target_pairs={{0,16},{2,18},{4,20},{6,22},{8,24},{10,26},{12,28},{14,30},{16,0},... | collective-permute-start | bytes 208904 | tf_op jit(solution)/shard_map/ppermute | solution.py:427
  32.4 3.8 %collective-permute-done.9 = bf16[272,128]{1,0:T(8,128)(2,1)S(1)} collective-permute-done((bf16[272,128]{1,0:T(8,128)(2,1)S(1)}, bf16[272,128]{1,0:T(8,128)(2,1)S(1)}, u32[]{:S(2)}, u32[]{:S(2)}) %collective-permute-start.9) | collective-permute-done | bytes 69664 | tf_op jit(solution)/shard_map/ppermute | solution.py:427
  36.2 1.0 %collective-permute-start.14 = (bf16[544,128]{1,0:T(8,128)(2,1)S(1)}, bf16[544,128]{1,0:T(8,128)(2,1)S(1)}, u32[]{:S(2)}, u32[]{:S(2)}) collective-permute-start(bf16[544,128]{1,0:T(8,128)(2,1)S(1)} %constant_dynamic-update-slice_fusion.refs_0_), channel_id=1, source_target_pairs={{0,4},{2,10},{4,0},{6,14},{8,12},{10,2},{12,8},{14,6},{16,20},{18,... | collective-permute-start | bytes 417800 | tf_op jit(solution)/shard_map/ppermute | solution.py:427
  37.2 0.4 collective-permute-start.11
  37.6 3.9 %collective-permute-done.11 = bf16[272,128]{1,0:T(8,128)(2,1)S(1)} collective-permute-done((bf16[272,128]{1,0:T(8,128)(2,1)S(1)}, bf16[272,128]{1,0:T(8,128)(2,1)S(1)}, u32[]{:S(2)}, u32[]{:S(2)}) %collective-permute-start.11) | collective-permute-done | bytes 69664 | tf_op jit(solution)/shard_map/ppermute | solution.py:427
  41.5 1.6 %collective-permute-start.15 = (bf16[544,128]{1,0:T(8,128)(2,1)S(1)}, bf16[544,128]{1,0:T(8,128)(2,1)S(1)}, u32[]{:S(2)}, u32[]{:S(2)}) collective-permute-start(bf16[544,128]{1,0:T(8,128)(2,1)S(1)} %constant_dynamic-update-slice_fusion.2.refs_1_), channel_id=1, source_target_pairs={{0,4},{2,10},{4,0},{6,14},{8,12},{10,2},{12,8},{14,6},{16,20},{18,... | collective-permute-start | bytes 417800 | tf_op jit(solution)/shard_map/ppermute | solution.py:427
  43.1 1.5 %collective-permute-start.13 = (bf16[4,16,128]{2,1,0:T(8,128)(2,1)S(1)}, bf16[4,16,128]{2,1,0:T(8,128)(2,1)S(1)}, u32[]{:S(2)}, u32[]{:S(2)}) collective-permute-start(bf16[4,16,128]{2,1,0:T(8,128)(2,1)S(1)} %pad_maximum_fusion.1), channel_id=1, source_target_pairs={{0,5},{1,4},{2,11},{3,10},{4,1},{5,0},{6,15},{7,14},{8,13},{9,12},... | collective-permute-start | bytes 49160 | tf_op jit(solution)/shard_map/ppermute | solution.py:435
  44.6 0.5 collective-permute-start.17
  45.1 1.5 %collective-permute-done.15.refs_3_ = bf16[544,128]{1,0:T(8,128)(2,1)S(1)} collective-permute-done((bf16[544,128]{1,0:T(8,128)(2,1)S(1)}, bf16[544,128]{1,0:T(8,128)(2,1)S(1)}, u32[]{:S(2)}, u32[]{:S(2)}) %collective-permute-start.15) | collective-permute-done | bytes 139296 | tf_op jit(solution)/shard_map/ppermute | solution.py:427
  46.6 1.2 %collective-permute-done.13 = bf16[4,16,128]{2,1,0:T(8,128)(2,1)S(1)} collective-permute-done((bf16[4,16,128]{2,1,0:T(8,128)(2,1)S(1)}, bf16[4,16,128]{2,1,0:T(8,128)(2,1)S(1)}, u32[]{:S(2)}, u32[]{:S(2)}) %collective-permute-start.13) | collective-permute-done | bytes 16416 | tf_op jit(solution)/shard_map/ppermute | solution.py:435
  47.8 1.5 %collective-permute-start.12 = (bf16[4,16,128]{2,1,0:T(8,128)(2,1)S(1)}, bf16[4,16,128]{2,1,0:T(8,128)(2,1)S(1)}, u32[]{:S(2)}, u32[]{:S(2)}) collective-permute-start(bf16[4,16,128]{2,1,0:T(8,128)(2,1)S(1)} %pad_maximum_fusion.1), channel_id=1, source_target_pairs={{0,1},{1,0},{2,3},{3,2},{4,5},{5,4},{6,7},{7,6},{8,9},{9,8},{10,11... | collective-permute-start | bytes 49160 | tf_op jit(solution)/shard_map/ppermute | solution.py:435
  49.3 3.1 %momentum_update.1.refs_8_ = bf16[128,8192]{1,0:T(8,128)(2,1)S(1)} custom-call(s32[1,64]{1,0:T(1,128)S(1)} %copy-done.4, bf16[128,8192]{1,0:T(8,128)(2,1)S(1)} %get-tuple-element.27.momentum_ref, bf16[2,128,8192]{2,1,0:T(8,128)(2,1)S(1)} %get-tuple-element.28.grads_ref, f32[2048,128]{1,0:T(8,128)S(1)} %get-tuple-element.29.taken_ref, ...), custom_call_target="tpu_custom_call" | custom-call | tf_op jit(solution)/shard_map/momentum_update/pallas_call | solution.py:264
  52.5 5.5 %weights_update.1 = (bf16[128,8192]{1,0:T(8,128)(2,1)}, f32[2]{0:T(128)}, bf16[128,8192]{1,0:T(8,128)(2,1)}, f32[4,32,128]{2,1,0:T(8,128)}, f32[4,32,128]{2,1,0:T(8,128)}) custom-call(s32[1,64]{1,0:T(1,128)S(1)} %copy-done.4, s32[1,64]{1,0:T(1,128)S(1)} %copy-done.5, bf16[1,8,16,128]{3,2,1,0:T(8,128)(2,1)S(1)} %maximum_bitcast_fusion.tiles_ref, ...), custom_call_target="tpu_custom_call" | custom-call | tf_op jit(solution)/shard_map/weights_update/pallas_call | solution.py:406
  (42 shorter events, 0.4 us)
Async XLA Ops:
  6.7 1.7 %collective-permute-start.1 = (bf16[32,32,128]{2,1,0:T(8,128)(2,1)S(1)}, bf16[32,32,128]{2,1,0:T(8,128)(2,1)S(1)}, u32[]{:S(2)}, u32[]{:S(2)}) collective-permute-start(bf16[32,32,128]{2,1,0:T(8,128)(2,1)S(1)} %get-tuple-element.37), channel_id=1, source_target_pairs={{0,2},{2,0},{4,6},{6,4},{8,10},{10,8},{12,14},{14,12},{16,18},{18,... | collective-permute-start | bytes 786440 | tf_op jit(solution)/shard_map/ppermute | solution.py:427
  7.3 4.3 %collective-permute-start = (bf16[32,32,128]{2,1,0:T(8,128)(2,1)S(1)}, bf16[32,32,128]{2,1,0:T(8,128)(2,1)S(1)}, u32[]{:S(2)}, u32[]{:S(2)}) collective-permute-start(bf16[32,32,128]{2,1,0:T(8,128)(2,1)S(1)} %get-tuple-element.38), channel_id=1, source_target_pairs={{0,2},{2,0},{4,6},{6,4},{8,10},{10,8},{12,14},{14,12},{16,18},{18,... | collective-permute-start | bytes 786440 | tf_op jit(solution)/shard_map/ppermute | solution.py:427
  8.4 15.0 %copy-start.2 = (f32[1,4,32,128]{3,2,1,0:T(8,128)S(1)}, f32[1,4,32,128]{3,2,1,0:T(8,128)}, u32[]{:S(2)}) copy-start(f32[1,4,32,128]{3,2,1,0:T(8,128)} %param.14) | copy-start | bytes 196612
  8.4 15.0 %copy-start.3 = (f32[1,4,32,128]{3,2,1,0:T(8,128)S(1)}, f32[1,4,32,128]{3,2,1,0:T(8,128)}, u32[]{:S(2)}) copy-start(f32[1,4,32,128]{3,2,1,0:T(8,128)} %param.15) | copy-start | bytes 196612
  8.5 5.9 %collective-permute-start.3 = (bf16[16,32,128]{2,1,0:T(8,128)(2,1)S(1)}, bf16[16,32,128]{2,1,0:T(8,128)(2,1)S(1)}, u32[]{:S(2)}, u32[]{:S(2)}) collective-permute-start(bf16[16,32,128]{2,1,0:T(8,128)(2,1)S(1)} %get-tuple-element.39), channel_id=1, source_target_pairs={{0,4},{2,10},{4,0},{6,14},{8,12},{10,2},{12,8},{14,6},{16,20},{18,... | collective-permute-start | bytes 393224 | tf_op jit(solution)/shard_map/ppermute | solution.py:427
  11.5 37.8 %copy-start = (bf16[3,256,256]{2,1,0:T(8,128)(2,1)S(1)}, bf16[3,256,256]{2,1,0:T(8,128)(2,1)}, u32[]{:S(2)}) copy-start(bf16[3,256,256]{2,1,0:T(8,128)(2,1)} %constant.5.clone.columns_hbm.columns_ref) | copy-start | bytes 1179652
  11.5 37.8 %copy-start.4 = (s32[1,64]{1,0:T(1,128)S(1)}, s32[1,64]{1,0:T(1,128)}, u32[]{:S(2)}) copy-start(s32[1,64]{1,0:T(1,128)} %offsets_ref.3) | copy-start | bytes 772
  11.5 5.0 %collective-permute-start.2 = (bf16[16,32,128]{2,1,0:T(8,128)(2,1)S(1)}, bf16[16,32,128]{2,1,0:T(8,128)(2,1)S(1)}, u32[]{:S(2)}, u32[]{:S(2)}) collective-permute-start(bf16[16,32,128]{2,1,0:T(8,128)(2,1)S(1)} %get-tuple-element.40), channel_id=1, source_target_pairs={{0,4},{2,10},{4,0},{6,14},{8,12},{10,2},{12,8},{14,6},{16,20},{18,... | collective-permute-start | bytes 393224 | tf_op jit(solution)/shard_map/ppermute | solution.py:427
  16.4 4.3 %collective-permute-start.5 = (bf16[8,32,128]{2,1,0:T(8,128)(2,1)S(1)}, bf16[8,32,128]{2,1,0:T(8,128)(2,1)S(1)}, u32[]{:S(2)}, u32[]{:S(2)}) collective-permute-start(bf16[8,32,128]{2,1,0:T(8,128)(2,1)S(1)} %get-tuple-element.42), channel_id=1, source_target_pairs={{0,8},{2,6},{4,12},{6,2},{8,0},{10,14},{12,4},{14,10},{16,24},{18,... | collective-permute-start | bytes 196616 | tf_op jit(solution)/shard_map/ppermute | solution.py:427
  18.0 5.4 %collective-permute-start.4 = (bf16[8,32,128]{2,1,0:T(8,128)(2,1)S(1)}, bf16[8,32,128]{2,1,0:T(8,128)(2,1)S(1)}, u32[]{:S(2)}, u32[]{:S(2)}) collective-permute-start(bf16[8,32,128]{2,1,0:T(8,128)(2,1)S(1)} %get-tuple-element.41), channel_id=1, source_target_pairs={{0,8},{2,6},{4,12},{6,2},{8,0},{10,14},{12,4},{14,10},{16,24},{18,... | collective-permute-start | bytes 196616 | tf_op jit(solution)/shard_map/ppermute | solution.py:427
  20.7 5.2 %collective-permute-start.6 = (bf16[8,32,128]{2,1,0:T(8,128)(2,1)S(1)}, bf16[8,32,128]{2,1,0:T(8,128)(2,1)S(1)}, u32[]{:S(2)}, u32[]{:S(2)}) collective-permute-start(bf16[8,32,128]{2,1,0:T(8,128)(2,1)S(1)} %slice_add_fusion.2), channel_id=1, source_target_pairs={{0,16},{2,18},{4,20},{6,22},{8,24},{10,26},{12,28},{14,30},{16,0},... | collective-permute-start | bytes 196616 | tf_op jit(solution)/shard_map/ppermute | solution.py:427
  23.4 2.7 %collective-permute-start.8 = (f32[2,4,32,128]{3,2,1,0:T(8,128)S(1)}, f32[2,4,32,128]{3,2,1,0:T(8,128)S(1)}, u32[]{:S(2)}, u32[]{:S(2)}) collective-permute-start(f32[2,4,32,128]{3,2,1,0:T(8,128)S(1)} %pad_maximum_fusion), channel_id=1, source_target_pairs={{0,2},{2,0},{4,6},{6,4},{8,10},{10,8},{12,14},{14,12},{16,18},{18,... | collective-permute-start | bytes 393224 | tf_op jit(solution)/shard_map/ppermute | solution.py:427
  26.0 1.4 %collective-permute-start.7 = (f32[8,32,128]{2,1,0:T(8,128)S(1)}, f32[8,32,128]{2,1,0:T(8,128)S(1)}, u32[]{:S(2)}, u32[]{:S(2)}) collective-permute-start(f32[8,32,128]{2,1,0:T(8,128)S(1)} %fusion.mine_ref), channel_id=1, source_target_pairs={{0,2},{2,0},{4,6},{6,4},{8,10},{10,8},{12,14},{14,12},{16,18},{18,... | collective-permute-start | bytes 393224 | tf_op jit(solution)/shard_map/ppermute | solution.py:427
  27.6 10.0 %collective-permute-start.10 = (bf16[272,128]{1,0:T(8,128)(2,1)S(1)}, bf16[272,128]{1,0:T(8,128)(2,1)S(1)}, u32[]{:S(2)}, u32[]{:S(2)}) collective-permute-start(bf16[272,128]{1,0:T(8,128)(2,1)S(1)} %get-tuple-element.26), channel_id=1, source_target_pairs={{0,8},{2,6},{4,12},{6,2},{8,0},{10,14},{12,4},{14,10},{16,24},{18,... | collective-permute-start | bytes 208904 | tf_op jit(solution)/shard_map/ppermute | solution.py:427
  29.2 7.0 %collective-permute-start.9 = (bf16[272,128]{1,0:T(8,128)(2,1)S(1)}, bf16[272,128]{1,0:T(8,128)(2,1)S(1)}, u32[]{:S(2)}, u32[]{:S(2)}) collective-permute-start(bf16[272,128]{1,0:T(8,128)(2,1)S(1)} %get-tuple-element.26), channel_id=1, source_target_pairs={{0,16},{2,18},{4,20},{6,22},{8,24},{10,26},{12,28},{14,30},{16,0},... | collective-permute-start | bytes 208904 | tf_op jit(solution)/shard_map/ppermute | solution.py:427
  36.2 8.9 %collective-permute-start.14 = (bf16[544,128]{1,0:T(8,128)(2,1)S(1)}, bf16[544,128]{1,0:T(8,128)(2,1)S(1)}, u32[]{:S(2)}, u32[]{:S(2)}) collective-permute-start(bf16[544,128]{1,0:T(8,128)(2,1)S(1)} %constant_dynamic-update-slice_fusion.refs_0_), channel_id=1, source_target_pairs={{0,4},{2,10},{4,0},{6,14},{8,12},{10,2},{12,8},{14,6},{16,20},{18,... | collective-permute-start | bytes 417800 | tf_op jit(solution)/shard_map/ppermute | solution.py:427
  37.2 4.3 %collective-permute-start.11 = (bf16[272,128]{1,0:T(8,128)(2,1)S(1)}, bf16[272,128]{1,0:T(8,128)(2,1)S(1)}, u32[]{:S(2)}, u32[]{:S(2)}) collective-permute-start(bf16[272,128]{1,0:T(8,128)(2,1)S(1)} %collective-permute-done.9), channel_id=1, source_target_pairs={{0,8},{2,6},{4,12},{6,2},{8,0},{10,14},{12,4},{14,10},{16,24},{18,... | collective-permute-start | bytes 208904 | tf_op jit(solution)/shard_map/ppermute | solution.py:427
  41.5 5.1 %collective-permute-start.15 = (bf16[544,128]{1,0:T(8,128)(2,1)S(1)}, bf16[544,128]{1,0:T(8,128)(2,1)S(1)}, u32[]{:S(2)}, u32[]{:S(2)}) collective-permute-start(bf16[544,128]{1,0:T(8,128)(2,1)S(1)} %constant_dynamic-update-slice_fusion.2.refs_1_), channel_id=1, source_target_pairs={{0,4},{2,10},{4,0},{6,14},{8,12},{10,2},{12,8},{14,6},{16,20},{18,... | collective-permute-start | bytes 417800 | tf_op jit(solution)/shard_map/ppermute | solution.py:427
  43.1 4.7 %collective-permute-start.13 = (bf16[4,16,128]{2,1,0:T(8,128)(2,1)S(1)}, bf16[4,16,128]{2,1,0:T(8,128)(2,1)S(1)}, u32[]{:S(2)}, u32[]{:S(2)}) collective-permute-start(bf16[4,16,128]{2,1,0:T(8,128)(2,1)S(1)} %pad_maximum_fusion.1), channel_id=1, source_target_pairs={{0,5},{1,4},{2,11},{3,10},{4,1},{5,0},{6,15},{7,14},{8,13},{9,12},... | collective-permute-start | bytes 49160 | tf_op jit(solution)/shard_map/ppermute | solution.py:435
  44.6 7.8 %collective-permute-start.16 = (bf16[544,128]{1,0:T(8,128)(2,1)S(1)}, bf16[544,128]{1,0:T(8,128)(2,1)S(1)}, u32[]{:S(2)}, u32[]{:S(2)}) collective-permute-start(bf16[544,128]{1,0:T(8,128)(2,1)S(1)} %constant_dynamic-update-slice_fusion.refs_0_), channel_id=1, source_target_pairs={{0,2},{2,0},{4,6},{6,4},{8,10},{10,8},{12,14},{14,12},{16,18},{18,... | collective-permute-start | bytes 417800 | tf_op jit(solution)/shard_map/ppermute | solution.py:427
  44.6 7.8 %collective-permute-start.17 = (bf16[544,128]{1,0:T(8,128)(2,1)S(1)}, bf16[544,128]{1,0:T(8,128)(2,1)S(1)}, u32[]{:S(2)}, u32[]{:S(2)}) collective-permute-start(bf16[544,128]{1,0:T(8,128)(2,1)S(1)} %constant_dynamic-update-slice_fusion.2.refs_1_), channel_id=1, source_target_pairs={{0,2},{2,0},{4,6},{6,4},{8,10},{10,8},{12,14},{14,12},{16,18},{18,... | collective-permute-start | bytes 417800 | tf_op jit(solution)/shard_map/ppermute | solution.py:427
  45.1 7.3 %collective-permute-start.18 = (bf16[544,128]{1,0:T(8,128)(2,1)S(1)}, bf16[544,128]{1,0:T(8,128)(2,1)S(1)}, u32[]{:S(2)}, u32[]{:S(2)}) collective-permute-start(bf16[544,128]{1,0:T(8,128)(2,1)S(1)} %collective-permute-done.14.refs_2_), channel_id=1, source_target_pairs={{0,2},{2,0},{4,6},{6,4},{8,10},{10,8},{12,14},{14,12},{16,18},{18,... | collective-permute-start | bytes 417800 | tf_op jit(solution)/shard_map/ppermute | solution.py:427
  46.6 5.8 %collective-permute-start.19 = (bf16[544,128]{1,0:T(8,128)(2,1)S(1)}, bf16[544,128]{1,0:T(8,128)(2,1)S(1)}, u32[]{:S(2)}, u32[]{:S(2)}) collective-permute-start(bf16[544,128]{1,0:T(8,128)(2,1)S(1)} %collective-permute-done.15.refs_3_), channel_id=1, source_target_pairs={{0,2},{2,0},{4,6},{6,4},{8,10},{10,8},{12,14},{14,12},{16,18},{18,... | collective-permute-start | bytes 417800 | tf_op jit(solution)/shard_map/ppermute | solution.py:427
  47.8 4.6 %collective-permute-start.12 = (bf16[4,16,128]{2,1,0:T(8,128)(2,1)S(1)}, bf16[4,16,128]{2,1,0:T(8,128)(2,1)S(1)}, u32[]{:S(2)}, u32[]{:S(2)}) collective-permute-start(bf16[4,16,128]{2,1,0:T(8,128)(2,1)S(1)} %pad_maximum_fusion.1), channel_id=1, source_target_pairs={{0,1},{1,0},{2,3},{3,2},{4,5},{5,4},{6,7},{7,6},{8,9},{9,8},{10,11... | collective-permute-start | bytes 49160 | tf_op jit(solution)/shard_map/ppermute | solution.py:435
  49.3 3.1 %copy-start.1 = (bf16[128,8192]{1,0:T(8,128)(2,1)S(1)}, bf16[128,8192]{1,0:T(8,128)(2,1)}, u32[]{:S(2)}) copy-start(bf16[128,8192]{1,0:T(8,128)(2,1)} %weights_ref.1) | copy-start | bytes 6291460
  49.3 3.1 %copy-start.5 = (s32[1,64]{1,0:T(1,128)S(1)}, s32[1,64]{1,0:T(1,128)}, u32[]{:S(2)}) copy-start(s32[1,64]{1,0:T(1,128)} %owners_ref.1) | copy-start | bytes 772

commit v3 on v2

--- a/solution.py
+++ b/solution.py
@@ -315,28 +315,81 @@
     )(*map(near_memory, (mine, got, exp_avg, exp_sq, others)))
 
 
-def weights_update(weights, own, other, tiles, count_all, offsets, owners, columns, ready, orders, band_rows, width):
+def gathered(piece_refs, groups_ref, owners_ref, target, row, block, geometry):
+    size, stride, owned, band_rows, row_blocks = geometry
+    shift = (size // stride).bit_length() - 1
+    owner, within = owner_of(owners_ref[row, block], owned)
+    group = groups_ref[target & 1, owner ^ target]
+    chip = group >> 1
+    which = chip >> shift
+    begin = (chip & ((1 << shift) - 1)) * stride + ((group & 1) * (row_blocks * owned) + row * owned + within) * band_rows
+    rows = pl.ds(pl.multiple_of(begin, TILE), band_rows)
+    value = piece_refs[0][rows, :]
+    for number in range(1, len(piece_refs)):
+        value = jnp.where(which == number, piece_refs[number][rows, :], value)
+    return value
+
+
+def exact_dot(values, table):
+    length = values.shape[1]
+    both = dot(values, table[:length])
+    return both[:, :length] + both[:, length:]
+
+
+def products_of(pieces, offsets, owners, columns, orders, band_rows, width):
+    row_blocks, col_blocks = offsets.shape
+    block_len = columns.shape[-1] // 2
+    chunks = col_blocks // width
+    geometry = (pieces[0].shape[0], 2 * pieces[0].shape[0] * len(pieces) >> len(orders[0]),
+                col_blocks >> len(orders[0]), band_rows, row_blocks)
+
+    def kernel(owners_ref, columns_ref, *refs):
+        *piece_refs, out_ref, groups_ref = refs
+        device = lax.axis_index("wide")
+        fill_groups(groups_ref, orders)
+
+        def body(part, carry):
+            row, chunk = block_of(part, chunks, row_blocks)
+            values = [gathered(piece_refs, groups_ref, owners_ref, device, row, chunk * width + index, geometry)
+                      for index in range(width)]
+            length = width * band_rows
+            out_ref[pl.ds(pl.multiple_of(part * length, length), length), :] = exact_dot(
+                jnp.concatenate(values, 0), columns_ref[0])
+            return carry
+
+        lax.fori_loop(0, row_blocks * chunks, body, 0)
+
+    return pl.pallas_call(
+        kernel,
+        in_specs=[SMEM] + [VMEM] * (1 + len(pieces)),
+        out_specs=VMEM,
+        out_shape=pltpu.VMEM((row_blocks * col_blocks * band_rows, block_len), jnp.float32),
+        scratch_shapes=[pltpu.SMEM((STEPS, 1 << len(orders[0])), jnp.int32)],
+        compiler_params=SMALL,
+        name="products_of",
+    )(owners, *map(near_memory, (columns, *pieces)))
+
+
+def weights_update(weights, own, products, other, tiles, count_all, offsets, owners, columns, ready, orders, band_rows, width):
     row_blocks, col_blocks = offsets.shape
     block_len = columns.shape[-1] // 2
     size = own[0].shape[0]
     pieces = len(own)
     stride = 2 * size * pieces >> len(orders[0])
-    shift = (size // stride).bit_length() - 1
     shards = tiles.shape[0] + 1
-    owned = col_blocks >> len(orders[0])
+    geometry = (size, stride, col_blocks >> len(orders[0]), band_rows, row_blocks)
     chunks = col_blocks // width
     span = width * block_len
     count = len(ready)
 
-    def kernel(offsets_ref, owners_ref, tiles_ref, weights_ref, columns_ref, *refs):
+    def kernel(offsets_ref, owners_ref, tiles_ref, weights_ref, columns_ref, products_ref, *refs):
         piece_refs = [refs[:pieces], refs[pieces:2 * pieces]]
         ready_refs = refs[2 * pieces:2 * pieces + count]
         refs = refs[2 * pieces + count:]
         out_hbm, scales_ref, ready_hbm = refs[0], refs[1], refs[2:2 + count]
         groups_ref, out_ref, departures, leaving, *scatters = refs[2 + count:]
-        device = lax.axis_index("wide")
-        role = device & 1
-        first_role = role == 0
+        partner = lax.axis_index("wide") ^ 1
+        first_role = (partner & 1) == 1
         copies = [
             pltpu.make_async_copy(source, target, leaving.at[index])
             for index, (source, target) in enumerate(zip(ready_refs, ready_hbm))
@@ -369,26 +422,15 @@
 
         def body(part, carry):
             row, chunk = block_of(part, chunks, row_blocks)
-            totals = []
-            for index in range(width):
-                slot = owners_ref[row, chunk * width + index]
-                owner, within = owner_of(slot, owned)
-                within = (row * owned + within) * band_rows
-                total = jnp.zeros((band_rows, block_len), jnp.float32)
-                for number in range(STEPS):
-                    group = groups_ref[role ^ number, owner ^ device ^ number]
-                    chip = group >> 1
-                    which = chip >> shift
-                    begin = (chip & ((1 << shift) - 1)) * stride + (group & 1) * (row_blocks * owned * band_rows) + within
-                    rows = pl.ds(pl.multiple_of(begin, TILE), band_rows)
-                    raw = piece_refs[number][0][rows, :]
-                    for piece in range(1, pieces):
-                        raw = jnp.where(which == piece, piece_refs[number][piece][rows, :], raw)
-                    total = total + raw.astype(jnp.float32) * factors[number]
-                totals.append(total)
-            right = right_dot(jnp.concatenate(totals, 0), columns_ref[0])
+            values = [gathered(piece_refs[1], groups_ref, owners_ref, partner, row, chunk * width + index, geometry)
+                      for index in range(width)]
+            right = exact_dot(jnp.concatenate(values, 0), columns_ref[0])
+            length = width * band_rows
+            start = pl.multiple_of(part * length, length)
             ranges = [pl.ds(offsets_ref[row, chunk * width + index], band_rows) for index in range(width)]
-            values = [right[index * band_rows:(index + 1) * band_rows] for index in range(width)]
+            values = [
+                products_ref[pl.ds(pl.multiple_of(start + index * band_rows, band_rows), band_rows), :] * factors[0]
+                + right[index * band_rows:(index + 1) * band_rows] * factors[1] for index in range(width)]
             inverse = left_dot(columns_ref, scatters, ranges, values)
             tile = tile_of(part)
             out_ref[tile] = (weights_ref[tile].astype(jnp.float32) - learning_rate * inverse).astype(out_ref.dtype)
@@ -405,7 +447,7 @@
 
     return pl.pallas_call(
         kernel,
-        in_specs=[SMEM, SMEM] + [VMEM] * (3 + 2 * pieces + count),
+        in_specs=[SMEM, SMEM] + [VMEM] * (4 + 2 * pieces + count),
         out_specs=[HBM, SMEM] + [HBM] * count,
         out_shape=[
             pltpu.HBM(weights.shape, weights.dtype),
@@ -419,7 +461,7 @@
         ] + [pltpu.VMEM((block_len, block_len), jnp.float32)] * (2 * width),
         compiler_params=SMALL,
         name="weights_update",
-    )(offsets, owners, *map(near_memory, (tiles, weights, columns, *own, *other, *ready)))
+    )(offsets, owners, *map(near_memory, (tiles, weights, columns, products, *own, *other, *ready)))
 
 
 def swap(value, orders, stage):
@@ -503,8 +545,9 @@
         for shift in range(1, shards)])
     own = nears + fars
     other = [swap(value, orders, core) for value in own]
+    products = products_of(own, offsets, owners, columns, orders, band_rows, 2 * width)
     new_weights, scales, new_momentum, avg_now, sq_now = weights_update(
-        weights, own, other, tiles, count_all, offsets, owners, columns, (new_momentum, avg_now, sq_now), orders, band_rows, width)
+        weights, own, products, other, tiles, count_all, offsets, owners, columns, (new_momentum, avg_now, sq_now), orders, band_rows, 2 * width)
     return (new_weights, new_momentum[None], avg_now.reshape(exp_avg.shape), sq_now.reshape(exp_sq.shape), scales)
 
 

time: 58.1 us -> 58.9 us (1.014)
  Pallas kernels: 14.8 us -> 15.5 us
    pallas_call x1 -> x2, Pallas kernels: 5.52 us -> 6.24 us  [the longest x1 4.81 us: weights_update(): pl.pallas_call(kernel, in_specs=[SMEM, SMEM] + [VMEM] * (4 + 2 * pieces +...]
  transfers between devices with their start and end apart: 20 -> 20, of which waited for: 10 -> 10; matrix products, arithmetic and copies ran while one was open for 1% -> 1% of each run, Pallas kernels for 5% -> 8%
where the time goes in v3:
time: 58.9 us; the launch traced here: 58.7 us
  waiting for transfers between devices  22.2 us (38%)
  starting transfers between devices  19.8 us (34%)
  Pallas kernels  15.5 us (26%)
  between operations  0.84 us (1%)
    ppermute x18, waiting for transfers between devices, swap(): return lax.ppermute(value, 'wide', pairs)  21 us
    ppermute x18, starting transfers between devices, swap(): return lax.ppermute(value, 'wide', pairs)  16.9 us
    pallas_call x1, Pallas kernels, bands(): pl.pallas_call(kernel, in_specs=[HBM] * 6, out_specs=[VMEM] * 5, out_shap...  6.02 us
    pallas_call x1, Pallas kernels, weights_update(): pl.pallas_call(kernel, in_specs=[SMEM, SMEM] + [VMEM] * (4 + 2 * pieces +...  4.81 us
    pallas_call x1, Pallas kernels, momentum_update(): pl.pallas_call(kernel, in_specs=[SMEM] + [VMEM] * 4, out_specs=VMEM, out_...  3.04 us
    ppermute x2, starting transfers between devices, across(): return lax.ppermute(value, ('wide', 'shard'), pairs)  2.94 us
    pallas_call x1, Pallas kernels, products_of(): pl.pallas_call(kernel, in_specs=[SMEM] + [VMEM] * (1 + len(pieces)), out_...  1.43 us
    ppermute x2, waiting for transfers between devices, across(): return lax.ppermute(value, ('wide', 'shard'), pairs)  1.18 us
  transfers between devices with their start and end apart: 20, of which 10 were waited for; matrix products, arithmetic and copies ran while one was open for 1% of the time, Pallas kernels for 8%

profile of v3, /device:TPU:0, one launch (start us, length us, event | category | flops | bytes accessed | tf_op | source)
XLA Modules:
  0.0 58.7 jit_solution(11403564492652444691)
XLA Ops:
  0.6 6.0 %bands.1 = (bf16[128,8192]{1,0:T(8,128)(2,1)S(1)}, bf16[2,128,8192]{2,1,0:T(8,128)(2,1)S(1)}, f32[2048,128]{1,0:T(8,128)S(1)}, f32[64,32,128]{2,1,0:T(8,128)S(1)}, bf16[64,32,128]{2,1,0:T(8,128)(2,1)S(1)}) custom-call(s32[1,64]{1,0:T(1,128)} %offsets_ref.3, s32[1,64]{1,0:T(1,128)} %owners_ref.3, bf16[128,8192]{1,0:T(8,128)(2,1)} %bitcast.16, ...), custom_call_target="tpu_custom_call" | custom-call | tf_op jit(solution)/shard_map/bands/pallas_call | solution.py:189
  6.7 0.6 collective-permute-start.1
  7.3 0.1 collective-permute-start
  7.3 1.1 %collective-permute-done.1 = bf16[32,32,128]{2,1,0:T(8,128)(2,1)S(1)} collective-permute-done((bf16[32,32,128]{2,1,0:T(8,128)(2,1)S(1)}, bf16[32,32,128]{2,1,0:T(8,128)(2,1)S(1)}, u32[]{:S(2)}, u32[]{:S(2)}) %collective-permute-start.1) | collective-permute-done | bytes 262176 | tf_op jit(solution)/shard_map/ppermute | solution.py:469
  8.4 0.1 convert_add_fusion.1
  8.5 2.9 %collective-permute-start.3 = (bf16[16,32,128]{2,1,0:T(8,128)(2,1)S(1)}, bf16[16,32,128]{2,1,0:T(8,128)(2,1)S(1)}, u32[]{:S(2)}, u32[]{:S(2)}) collective-permute-start(bf16[16,32,128]{2,1,0:T(8,128)(2,1)S(1)} %get-tuple-element.39), channel_id=1, source_target_pairs={{0,4},{2,10},{4,0},{6,14},{8,12},{10,2},{12,8},{14,6},{16,20},{18,... | collective-permute-start | bytes 393224 | tf_op jit(solution)/shard_map/ppermute | solution.py:469
  11.5 0.1 collective-permute-start.2
  11.7 2.8 %collective-permute-done.3 = bf16[16,32,128]{2,1,0:T(8,128)(2,1)S(1)} collective-permute-done((bf16[16,32,128]{2,1,0:T(8,128)(2,1)S(1)}, bf16[16,32,128]{2,1,0:T(8,128)(2,1)S(1)}, u32[]{:S(2)}, u32[]{:S(2)}) %collective-permute-start.3) | collective-permute-done | bytes 131104 | tf_op jit(solution)/shard_map/ppermute | solution.py:469
  14.5 2.0 %collective-permute-done.2 = bf16[16,32,128]{2,1,0:T(8,128)(2,1)S(1)} collective-permute-done((bf16[16,32,128]{2,1,0:T(8,128)(2,1)S(1)}, bf16[16,32,128]{2,1,0:T(8,128)(2,1)S(1)}, u32[]{:S(2)}, u32[]{:S(2)}) %collective-permute-start.2) | collective-permute-done | bytes 131104 | tf_op jit(solution)/shard_map/ppermute | solution.py:469
  16.4 1.6 %collective-permute-start.5 = (bf16[8,32,128]{2,1,0:T(8,128)(2,1)S(1)}, bf16[8,32,128]{2,1,0:T(8,128)(2,1)S(1)}, u32[]{:S(2)}, u32[]{:S(2)}) collective-permute-start(bf16[8,32,128]{2,1,0:T(8,128)(2,1)S(1)} %get-tuple-element.42), channel_id=1, source_target_pairs={{0,8},{2,6},{4,12},{6,2},{8,0},{10,14},{12,4},{14,10},{16,24},{18,... | collective-permute-start | bytes 196616 | tf_op jit(solution)/shard_map/ppermute | solution.py:469
  18.1 0.5 collective-permute-start.4
  18.6 2.1 %collective-permute-done.5 = bf16[8,32,128]{2,1,0:T(8,128)(2,1)S(1)} collective-permute-done((bf16[8,32,128]{2,1,0:T(8,128)(2,1)S(1)}, bf16[8,32,128]{2,1,0:T(8,128)(2,1)S(1)}, u32[]{:S(2)}, u32[]{:S(2)}) %collective-permute-start.5) | collective-permute-done | bytes 65568 | tf_op jit(solution)/shard_map/ppermute | solution.py:469
  20.7 2.7 %collective-permute-start.6 = (bf16[8,32,128]{2,1,0:T(8,128)(2,1)S(1)}, bf16[8,32,128]{2,1,0:T(8,128)(2,1)S(1)}, u32[]{:S(2)}, u32[]{:S(2)}) collective-permute-start(bf16[8,32,128]{2,1,0:T(8,128)(2,1)S(1)} %slice_add_fusion.2), channel_id=1, source_target_pairs={{0,16},{2,18},{4,20},{6,22},{8,24},{10,26},{12,28},{14,30},{16,0},... | collective-permute-start | bytes 196616 | tf_op jit(solution)/shard_map/ppermute | solution.py:469
  23.4 0.1 collective-permute-start.8
  23.5 2.5 %collective-permute-done.6 = bf16[8,32,128]{2,1,0:T(8,128)(2,1)S(1)} collective-permute-done((bf16[8,32,128]{2,1,0:T(8,128)(2,1)S(1)}, bf16[8,32,128]{2,1,0:T(8,128)(2,1)S(1)}, u32[]{:S(2)}, u32[]{:S(2)}) %collective-permute-start.6) | collective-permute-done | bytes 65568 | tf_op jit(solution)/shard_map/ppermute | solution.py:469
  26.1 1.3 %collective-permute-done.7.got_ref = f32[8,32,128]{2,1,0:T(8,128)S(1)} collective-permute-done((f32[8,32,128]{2,1,0:T(8,128)S(1)}, f32[8,32,128]{2,1,0:T(8,128)S(1)}, u32[]{:S(2)}, u32[]{:S(2)}) %collective-permute-start.7) | collective-permute-done | bytes 131104 | tf_op jit(solution)/shard_map/ppermute | solution.py:469
  27.4 0.2 adam.1
  27.6 1.6 %collective-permute-start.10 = (bf16[272,128]{1,0:T(8,128)(2,1)S(1)}, bf16[272,128]{1,0:T(8,128)(2,1)S(1)}, u32[]{:S(2)}, u32[]{:S(2)}) collective-permute-start(bf16[272,128]{1,0:T(8,128)(2,1)S(1)} %get-tuple-element.26), channel_id=1, source_target_pairs={{0,8},{2,6},{4,12},{6,2},{8,0},{10,14},{12,4},{14,10},{16,24},{18,... | collective-permute-start | bytes 208904 | tf_op jit(solution)/shard_map/ppermute | solution.py:469
  29.3 3.2 %collective-permute-start.9 = (bf16[272,128]{1,0:T(8,128)(2,1)S(1)}, bf16[272,128]{1,0:T(8,128)(2,1)S(1)}, u32[]{:S(2)}, u32[]{:S(2)}) collective-permute-start(bf16[272,128]{1,0:T(8,128)(2,1)S(1)} %get-tuple-element.26), channel_id=1, source_target_pairs={{0,16},{2,18},{4,20},{6,22},{8,24},{10,26},{12,28},{14,30},{16,0},... | collective-permute-start | bytes 208904 | tf_op jit(solution)/shard_map/ppermute | solution.py:469
  32.4 3.8 %collective-permute-done.9 = bf16[272,128]{1,0:T(8,128)(2,1)S(1)} collective-permute-done((bf16[272,128]{1,0:T(8,128)(2,1)S(1)}, bf16[272,128]{1,0:T(8,128)(2,1)S(1)}, u32[]{:S(2)}, u32[]{:S(2)}) %collective-permute-start.9) | collective-permute-done | bytes 69664 | tf_op jit(solution)/shard_map/ppermute | solution.py:469
  36.2 1.0 %collective-permute-start.14 = (bf16[544,128]{1,0:T(8,128)(2,1)S(1)}, bf16[544,128]{1,0:T(8,128)(2,1)S(1)}, u32[]{:S(2)}, u32[]{:S(2)}) collective-permute-start(bf16[544,128]{1,0:T(8,128)(2,1)S(1)} %constant_dynamic-update-slice_fusion.refs_0_), channel_id=1, source_target_pairs={{0,4},{2,10},{4,0},{6,14},{8,12},{10,2},{12,8},{14,6},{16,20},{18,... | collective-permute-start | bytes 417800 | tf_op jit(solution)/shard_map/ppermute | solution.py:469
  37.2 0.4 collective-permute-start.11
  37.6 3.9 %collective-permute-done.11 = bf16[272,128]{1,0:T(8,128)(2,1)S(1)} collective-permute-done((bf16[272,128]{1,0:T(8,128)(2,1)S(1)}, bf16[272,128]{1,0:T(8,128)(2,1)S(1)}, u32[]{:S(2)}, u32[]{:S(2)}) %collective-permute-start.11) | collective-permute-done | bytes 69664 | tf_op jit(solution)/shard_map/ppermute | solution.py:469
  41.5 1.6 %collective-permute-start.15 = (bf16[544,128]{1,0:T(8,128)(2,1)S(1)}, bf16[544,128]{1,0:T(8,128)(2,1)S(1)}, u32[]{:S(2)}, u32[]{:S(2)}) collective-permute-start(bf16[544,128]{1,0:T(8,128)(2,1)S(1)} %constant_dynamic-update-slice_fusion.2.refs_1_), channel_id=1, source_target_pairs={{0,4},{2,10},{4,0},{6,14},{8,12},{10,2},{12,8},{14,6},{16,20},{18,... | collective-permute-start | bytes 417800 | tf_op jit(solution)/shard_map/ppermute | solution.py:469
  43.1 1.5 %collective-permute-start.13 = (bf16[4,16,128]{2,1,0:T(8,128)(2,1)S(1)}, bf16[4,16,128]{2,1,0:T(8,128)(2,1)S(1)}, u32[]{:S(2)}, u32[]{:S(2)}) collective-permute-start(bf16[4,16,128]{2,1,0:T(8,128)(2,1)S(1)} %pad_maximum_fusion.1), channel_id=1, source_target_pairs={{0,5},{1,4},{2,11},{3,10},{4,1},{5,0},{6,15},{7,14},{8,13},{9,12},... | collective-permute-start | bytes 49160 | tf_op jit(solution)/shard_map/ppermute | solution.py:477
  44.6 0.5 collective-permute-start.17
  45.1 1.5 %collective-permute-done.15.refs_3_ = bf16[544,128]{1,0:T(8,128)(2,1)S(1)} collective-permute-done((bf16[544,128]{1,0:T(8,128)(2,1)S(1)}, bf16[544,128]{1,0:T(8,128)(2,1)S(1)}, u32[]{:S(2)}, u32[]{:S(2)}) %collective-permute-start.15) | collective-permute-done | bytes 139296 | tf_op jit(solution)/shard_map/ppermute | solution.py:469
  46.7 1.2 %collective-permute-done.13 = bf16[4,16,128]{2,1,0:T(8,128)(2,1)S(1)} collective-permute-done((bf16[4,16,128]{2,1,0:T(8,128)(2,1)S(1)}, bf16[4,16,128]{2,1,0:T(8,128)(2,1)S(1)}, u32[]{:S(2)}, u32[]{:S(2)}) %collective-permute-start.13) | collective-permute-done | bytes 16416 | tf_op jit(solution)/shard_map/ppermute | solution.py:477
  47.8 1.5 %collective-permute-start.12 = (bf16[4,16,128]{2,1,0:T(8,128)(2,1)S(1)}, bf16[4,16,128]{2,1,0:T(8,128)(2,1)S(1)}, u32[]{:S(2)}, u32[]{:S(2)}) collective-permute-start(bf16[4,16,128]{2,1,0:T(8,128)(2,1)S(1)} %pad_maximum_fusion.1), channel_id=1, source_target_pairs={{0,1},{1,0},{2,3},{3,2},{4,5},{5,4},{6,7},{7,6},{8,9},{9,8},{10,11... | collective-permute-start | bytes 49160 | tf_op jit(solution)/shard_map/ppermute | solution.py:477
  49.3 3.0 %momentum_update.1.refs_8_ = bf16[128,8192]{1,0:T(8,128)(2,1)S(1)} custom-call(s32[1,64]{1,0:T(1,128)S(1)} %copy-done.4, bf16[128,8192]{1,0:T(8,128)(2,1)S(1)} %get-tuple-element.27.momentum_ref, bf16[2,128,8192]{2,1,0:T(8,128)(2,1)S(1)} %get-tuple-element.28.grads_ref, f32[2048,128]{1,0:T(8,128)S(1)} %get-tuple-element.29.taken_ref, ...), custom_call_target="tpu_custom_call" | custom-call | tf_op jit(solution)/shard_map/momentum_update/pallas_call | solution.py:264
  52.4 1.4 %products_of.1.products_ref = f32[2048,128]{1,0:T(8,128)S(1)} custom-call(s32[1,64]{1,0:T(1,128)S(1)} %copy-done.5, bf16[3,256,256]{2,1,0:T(8,128)(2,1)S(1)} %copy-done, bf16[544,128]{1,0:T(8,128)(2,1)S(1)} %constant_dynamic-update-slice_fusion.refs_0_, bf16[544,128]{1,0:T(8,128)(2,1)S(1)} %constant_dynamic-update-slice_fusion.2.refs_1_, ...), custom_call_target="tpu_custom_call" | custom-call | tf_op jit(solution)/shard_map/products_of/pallas_call | solution.py:362
  53.9 4.8 %weights_update.1 = (bf16[128,8192]{1,0:T(8,128)(2,1)}, f32[2]{0:T(128)}, bf16[128,8192]{1,0:T(8,128)(2,1)}, f32[4,32,128]{2,1,0:T(8,128)}, f32[4,32,128]{2,1,0:T(8,128)}) custom-call(s32[1,64]{1,0:T(1,128)S(1)} %copy-done.4, s32[1,64]{1,0:T(1,128)S(1)} %copy-done.5, bf16[1,8,16,128]{3,2,1,0:T(8,128)(2,1)S(1)} %maximum_bitcast_fusion.tiles_ref, ...), custom_call_target="tpu_custom_call" | custom-call | tf_op jit(solution)/shard_map/weights_update/pallas_call | solution.py:448
  (43 shorter events, 0.4 us)
Async XLA Ops:
  6.7 1.7 %collective-permute-start.1 = (bf16[32,32,128]{2,1,0:T(8,128)(2,1)S(1)}, bf16[32,32,128]{2,1,0:T(8,128)(2,1)S(1)}, u32[]{:S(2)}, u32[]{:S(2)}) collective-permute-start(bf16[32,32,128]{2,1,0:T(8,128)(2,1)S(1)} %get-tuple-element.37), channel_id=1, source_target_pairs={{0,2},{2,0},{4,6},{6,4},{8,10},{10,8},{12,14},{14,12},{16,18},{18,... | collective-permute-start | bytes 786440 | tf_op jit(solution)/shard_map/ppermute | solution.py:469
  7.3 4.3 %collective-permute-start = (bf16[32,32,128]{2,1,0:T(8,128)(2,1)S(1)}, bf16[32,32,128]{2,1,0:T(8,128)(2,1)S(1)}, u32[]{:S(2)}, u32[]{:S(2)}) collective-permute-start(bf16[32,32,128]{2,1,0:T(8,128)(2,1)S(1)} %get-tuple-element.38), channel_id=1, source_target_pairs={{0,2},{2,0},{4,6},{6,4},{8,10},{10,8},{12,14},{14,12},{16,18},{18,... | collective-permute-start | bytes 786440 | tf_op jit(solution)/shard_map/ppermute | solution.py:469
  8.4 15.0 %copy-start.2 = (f32[1,4,32,128]{3,2,1,0:T(8,128)S(1)}, f32[1,4,32,128]{3,2,1,0:T(8,128)}, u32[]{:S(2)}) copy-start(f32[1,4,32,128]{3,2,1,0:T(8,128)} %param.14) | copy-start | bytes 196612
  8.4 15.0 %copy-start.3 = (f32[1,4,32,128]{3,2,1,0:T(8,128)S(1)}, f32[1,4,32,128]{3,2,1,0:T(8,128)}, u32[]{:S(2)}) copy-start(f32[1,4,32,128]{3,2,1,0:T(8,128)} %param.15) | copy-start | bytes 196612
  8.5 5.9 %collective-permute-start.3 = (bf16[16,32,128]{2,1,0:T(8,128)(2,1)S(1)}, bf16[16,32,128]{2,1,0:T(8,128)(2,1)S(1)}, u32[]{:S(2)}, u32[]{:S(2)}) collective-permute-start(bf16[16,32,128]{2,1,0:T(8,128)(2,1)S(1)} %get-tuple-element.39), channel_id=1, source_target_pairs={{0,4},{2,10},{4,0},{6,14},{8,12},{10,2},{12,8},{14,6},{16,20},{18,... | collective-permute-start | bytes 393224 | tf_op jit(solution)/shard_map/ppermute | solution.py:469
  11.5 37.9 %copy-start = (bf16[3,256,256]{2,1,0:T(8,128)(2,1)S(1)}, bf16[3,256,256]{2,1,0:T(8,128)(2,1)}, u32[]{:S(2)}) copy-start(bf16[3,256,256]{2,1,0:T(8,128)(2,1)} %constant.5.clone.columns_hbm.columns_ref) | copy-start | bytes 1179652
  11.5 37.9 %copy-start.4 = (s32[1,64]{1,0:T(1,128)S(1)}, s32[1,64]{1,0:T(1,128)}, u32[]{:S(2)}) copy-start(s32[1,64]{1,0:T(1,128)} %offsets_ref.3) | copy-start | bytes 772
  11.5 5.0 %collective-permute-start.2 = (bf16[16,32,128]{2,1,0:T(8,128)(2,1)S(1)}, bf16[16,32,128]{2,1,0:T(8,128)(2,1)S(1)}, u32[]{:S(2)}, u32[]{:S(2)}) collective-permute-start(bf16[16,32,128]{2,1,0:T(8,128)(2,1)S(1)} %get-tuple-element.40), channel_id=1, source_target_pairs={{0,4},{2,10},{4,0},{6,14},{8,12},{10,2},{12,8},{14,6},{16,20},{18,... | collective-permute-start | bytes 393224 | tf_op jit(solution)/shard_map/ppermute | solution.py:469
  16.4 4.3 %collective-permute-start.5 = (bf16[8,32,128]{2,1,0:T(8,128)(2,1)S(1)}, bf16[8,32,128]{2,1,0:T(8,128)(2,1)S(1)}, u32[]{:S(2)}, u32[]{:S(2)}) collective-permute-start(bf16[8,32,128]{2,1,0:T(8,128)(2,1)S(1)} %get-tuple-element.42), channel_id=1, source_target_pairs={{0,8},{2,6},{4,12},{6,2},{8,0},{10,14},{12,4},{14,10},{16,24},{18,... | collective-permute-start | bytes 196616 | tf_op jit(solution)/shard_map/ppermute | solution.py:469
  18.1 5.4 %collective-permute-start.4 = (bf16[8,32,128]{2,1,0:T(8,128)(2,1)S(1)}, bf16[8,32,128]{2,1,0:T(8,128)(2,1)S(1)}, u32[]{:S(2)}, u32[]{:S(2)}) collective-permute-start(bf16[8,32,128]{2,1,0:T(8,128)(2,1)S(1)} %get-tuple-element.41), channel_id=1, source_target_pairs={{0,8},{2,6},{4,12},{6,2},{8,0},{10,14},{12,4},{14,10},{16,24},{18,... | collective-permute-start | bytes 196616 | tf_op jit(solution)/shard_map/ppermute | solution.py:469
  20.7 5.2 %collective-permute-start.6 = (bf16[8,32,128]{2,1,0:T(8,128)(2,1)S(1)}, bf16[8,32,128]{2,1,0:T(8,128)(2,1)S(1)}, u32[]{:S(2)}, u32[]{:S(2)}) collective-permute-start(bf16[8,32,128]{2,1,0:T(8,128)(2,1)S(1)} %slice_add_fusion.2), channel_id=1, source_target_pairs={{0,16},{2,18},{4,20},{6,22},{8,24},{10,26},{12,28},{14,30},{16,0},... | collective-permute-start | bytes 196616 | tf_op jit(solution)/shard_map/ppermute | solution.py:469
  23.4 2.7 %collective-permute-start.8 = (f32[2,4,32,128]{3,2,1,0:T(8,128)S(1)}, f32[2,4,32,128]{3,2,1,0:T(8,128)S(1)}, u32[]{:S(2)}, u32[]{:S(2)}) collective-permute-start(f32[2,4,32,128]{3,2,1,0:T(8,128)S(1)} %pad_maximum_fusion), channel_id=1, source_target_pairs={{0,2},{2,0},{4,6},{6,4},{8,10},{10,8},{12,14},{14,12},{16,18},{18,... | collective-permute-start | bytes 393224 | tf_op jit(solution)/shard_map/ppermute | solution.py:469
  26.0 1.4 %collective-permute-start.7 = (f32[8,32,128]{2,1,0:T(8,128)S(1)}, f32[8,32,128]{2,1,0:T(8,128)S(1)}, u32[]{:S(2)}, u32[]{:S(2)}) collective-permute-start(f32[8,32,128]{2,1,0:T(8,128)S(1)} %fusion.mine_ref), channel_id=1, source_target_pairs={{0,2},{2,0},{4,6},{6,4},{8,10},{10,8},{12,14},{14,12},{16,18},{18,... | collective-permute-start | bytes 393224 | tf_op jit(solution)/shard_map/ppermute | solution.py:469
  27.6 10.0 %collective-permute-start.10 = (bf16[272,128]{1,0:T(8,128)(2,1)S(1)}, bf16[272,128]{1,0:T(8,128)(2,1)S(1)}, u32[]{:S(2)}, u32[]{:S(2)}) collective-permute-start(bf16[272,128]{1,0:T(8,128)(2,1)S(1)} %get-tuple-element.26), channel_id=1, source_target_pairs={{0,8},{2,6},{4,12},{6,2},{8,0},{10,14},{12,4},{14,10},{16,24},{18,... | collective-permute-start | bytes 208904 | tf_op jit(solution)/shard_map/ppermute | solution.py:469
  29.3 7.0 %collective-permute-start.9 = (bf16[272,128]{1,0:T(8,128)(2,1)S(1)}, bf16[272,128]{1,0:T(8,128)(2,1)S(1)}, u32[]{:S(2)}, u32[]{:S(2)}) collective-permute-start(bf16[272,128]{1,0:T(8,128)(2,1)S(1)} %get-tuple-element.26), channel_id=1, source_target_pairs={{0,16},{2,18},{4,20},{6,22},{8,24},{10,26},{12,28},{14,30},{16,0},... | collective-permute-start | bytes 208904 | tf_op jit(solution)/shard_map/ppermute | solution.py:469
  36.2 8.9 %collective-permute-start.14 = (bf16[544,128]{1,0:T(8,128)(2,1)S(1)}, bf16[544,128]{1,0:T(8,128)(2,1)S(1)}, u32[]{:S(2)}, u32[]{:S(2)}) collective-permute-start(bf16[544,128]{1,0:T(8,128)(2,1)S(1)} %constant_dynamic-update-slice_fusion.refs_0_), channel_id=1, source_target_pairs={{0,4},{2,10},{4,0},{6,14},{8,12},{10,2},{12,8},{14,6},{16,20},{18,... | collective-permute-start | bytes 417800 | tf_op jit(solution)/shard_map/ppermute | solution.py:469
  37.2 4.3 %collective-permute-start.11 = (bf16[272,128]{1,0:T(8,128)(2,1)S(1)}, bf16[272,128]{1,0:T(8,128)(2,1)S(1)}, u32[]{:S(2)}, u32[]{:S(2)}) collective-permute-start(bf16[272,128]{1,0:T(8,128)(2,1)S(1)} %collective-permute-done.9), channel_id=1, source_target_pairs={{0,8},{2,6},{4,12},{6,2},{8,0},{10,14},{12,4},{14,10},{16,24},{18,... | collective-permute-start | bytes 208904 | tf_op jit(solution)/shard_map/ppermute | solution.py:469
  41.5 5.1 %collective-permute-start.15 = (bf16[544,128]{1,0:T(8,128)(2,1)S(1)}, bf16[544,128]{1,0:T(8,128)(2,1)S(1)}, u32[]{:S(2)}, u32[]{:S(2)}) collective-permute-start(bf16[544,128]{1,0:T(8,128)(2,1)S(1)} %constant_dynamic-update-slice_fusion.2.refs_1_), channel_id=1, source_target_pairs={{0,4},{2,10},{4,0},{6,14},{8,12},{10,2},{12,8},{14,6},{16,20},{18,... | collective-permute-start | bytes 417800 | tf_op jit(solution)/shard_map/ppermute | solution.py:469
  43.1 4.7 %collective-permute-start.13 = (bf16[4,16,128]{2,1,0:T(8,128)(2,1)S(1)}, bf16[4,16,128]{2,1,0:T(8,128)(2,1)S(1)}, u32[]{:S(2)}, u32[]{:S(2)}) collective-permute-start(bf16[4,16,128]{2,1,0:T(8,128)(2,1)S(1)} %pad_maximum_fusion.1), channel_id=1, source_target_pairs={{0,5},{1,4},{2,11},{3,10},{4,1},{5,0},{6,15},{7,14},{8,13},{9,12},... | collective-permute-start | bytes 49160 | tf_op jit(solution)/shard_map/ppermute | solution.py:477
  44.6 9.2 %collective-permute-start.16 = (bf16[544,128]{1,0:T(8,128)(2,1)S(1)}, bf16[544,128]{1,0:T(8,128)(2,1)S(1)}, u32[]{:S(2)}, u32[]{:S(2)}) collective-permute-start(bf16[544,128]{1,0:T(8,128)(2,1)S(1)} %constant_dynamic-update-slice_fusion.refs_0_), channel_id=1, source_target_pairs={{0,2},{2,0},{4,6},{6,4},{8,10},{10,8},{12,14},{14,12},{16,18},{18,... | collective-permute-start | bytes 417800 | tf_op jit(solution)/shard_map/ppermute | solution.py:469
  44.6 9.3 %collective-permute-start.17 = (bf16[544,128]{1,0:T(8,128)(2,1)S(1)}, bf16[544,128]{1,0:T(8,128)(2,1)S(1)}, u32[]{:S(2)}, u32[]{:S(2)}) collective-permute-start(bf16[544,128]{1,0:T(8,128)(2,1)S(1)} %constant_dynamic-update-slice_fusion.2.refs_1_), channel_id=1, source_target_pairs={{0,2},{2,0},{4,6},{6,4},{8,10},{10,8},{12,14},{14,12},{16,18},{18,... | collective-permute-start | bytes 417800 | tf_op jit(solution)/shard_map/ppermute | solution.py:469
  45.1 8.8 %collective-permute-start.18 = (bf16[544,128]{1,0:T(8,128)(2,1)S(1)}, bf16[544,128]{1,0:T(8,128)(2,1)S(1)}, u32[]{:S(2)}, u32[]{:S(2)}) collective-permute-start(bf16[544,128]{1,0:T(8,128)(2,1)S(1)} %collective-permute-done.14.refs_2_), channel_id=1, source_target_pairs={{0,2},{2,0},{4,6},{6,4},{8,10},{10,8},{12,14},{14,12},{16,18},{18,... | collective-permute-start | bytes 417800 | tf_op jit(solution)/shard_map/ppermute | solution.py:469
  46.7 7.2 %collective-permute-start.19 = (bf16[544,128]{1,0:T(8,128)(2,1)S(1)}, bf16[544,128]{1,0:T(8,128)(2,1)S(1)}, u32[]{:S(2)}, u32[]{:S(2)}) collective-permute-start(bf16[544,128]{1,0:T(8,128)(2,1)S(1)} %collective-permute-done.15.refs_3_), channel_id=1, source_target_pairs={{0,2},{2,0},{4,6},{6,4},{8,10},{10,8},{12,14},{14,12},{16,18},{18,... | collective-permute-start | bytes 417800 | tf_op jit(solution)/shard_map/ppermute | solution.py:469
  47.8 4.5 %collective-permute-start.12 = (bf16[4,16,128]{2,1,0:T(8,128)(2,1)S(1)}, bf16[4,16,128]{2,1,0:T(8,128)(2,1)S(1)}, u32[]{:S(2)}, u32[]{:S(2)}) collective-permute-start(bf16[4,16,128]{2,1,0:T(8,128)(2,1)S(1)} %pad_maximum_fusion.1), channel_id=1, source_target_pairs={{0,1},{1,0},{2,3},{3,2},{4,5},{5,4},{6,7},{7,6},{8,9},{9,8},{10,11... | collective-permute-start | bytes 49160 | tf_op jit(solution)/shard_map/ppermute | solution.py:477
  49.3 3.1 %copy-start.5 = (s32[1,64]{1,0:T(1,128)S(1)}, s32[1,64]{1,0:T(1,128)}, u32[]{:S(2)}) copy-start(s32[1,64]{1,0:T(1,128)} %owners_ref.3) | copy-start | bytes 772
  49.3 4.6 %copy-start.1 = (bf16[128,8192]{1,0:T(8,128)(2,1)S(1)}, bf16[128,8192]{1,0:T(8,128)(2,1)}, u32[]{:S(2)}) copy-start(bf16[128,8192]{1,0:T(8,128)(2,1)} %weights_ref.1) | copy-start | bytes 6291460
